TPU v7x, 32 devices: a whole 2x2x4 slice. The times are simulated.
32 devices in a mesh: seq: 8 (over y, x, core), tp: 4 (over z).
Axes of the slice: x: 2, y: 2, z: 4, core: 2. Of those that a mesh axis runs over, the one named last changes fastest.
Arguments:
- tokens: bfloat16 [1, 8, 1024, 768], P(None, 'seq', 'tp'), may hold values from -6 to 6
- cotangent: bfloat16 [1, 8, 1024, 768], P(None, 'seq', 'tp'), may hold values from -6 to 6
- lengths: int32 [1], replicated, may hold values from 64 to 1024
- column_mask: int32 [1, 1024], replicated, may hold values 0 or 1
- row_gain: float32 [768], replicated, may hold values from 0.5 to 1.5
- row_qkv: bfloat16 [3, 768, 768], P(None, None, 'tp'), may hold values from -0.3125 to 0.3125
- row_out: bfloat16 [768, 768], P('tp'), may hold values from -0.625 to 0.625
- col_gain: float32 [768], replicated, may hold values from 0.5 to 1.5
- col_qkv: bfloat16 [3, 768, 768], P(None, None, 'tp'), may hold values from -0.21875 to 0.21875
- col_out: bfloat16 [768, 768], P('tp'), may hold values from -0.875 to 0.875
- ffn_gain: float32 [768], replicated, may hold values from 0.5 to 1.5
- ffn_up: bfloat16 [768, 3072], P(None, 'tp'), may hold values from -0.21875 to 0.21875
- ffn_down: bfloat16 [3072, 768], P('tp'), may hold values from -0.109375 to 0.109375
Outputs:
- activations: bfloat16 [1, 8, 1024, 768], P(None, 'seq', 'tp')
- input_grad: bfloat16 [1, 8, 1024, 768], P(None, 'seq', 'tp')
- row_gain_grad: float32 [768], replicated
- row_qkv_grad: float32 [3, 768, 768], P(None, 'seq', 'tp')
- row_out_grad: float32 [768, 768], P('tp', 'seq')
- col_gain_grad: float32 [768], replicated
- col_qkv_grad: float32 [3, 768, 768], P(None, 'seq', 'tp')
- col_out_grad: float32 [768, 768], P('tp', 'seq')
- ffn_gain_grad: float32 [768], replicated
- ffn_up_grad: float32 [768, 3072], P('seq', 'tp')
- ffn_down_grad: float32 [3072, 768], P('tp', 'seq')
All inputs are finite; a program needn't handle non-finite values.
Results may differ from a plain program's by a relative error of at most 0.025.
The roundings to bfloat16 on the way count: a program that leaves them out, or rounds other values in their place, can miss the bound.
Values may be sent and summed in bfloat16 or wider, within the bound.
No kernel may reach another device: no remote copies, remote signals or barrier semaphores. Data moves between devices by JAX's collectives and lax.ppermute only.
A program may use at most 192 MiB of HBM per device.

v0:
```python
import jax
import jax.numpy as jnp
from jax import lax
from jax.sharding import PartitionSpec as P

HEADS = 12
HEAD = 64


EPSILON = 1e-05
NEGATIVE = -1e30
ENTROPY_WEIGHT = 4.0


def layer_norm(skip_carry_tensor, norm_gain):
    average = jnp.mean(skip_carry_tensor, axis=-1, keepdims=True)
    centred = skip_carry_tensor - average
    spread = jnp.mean(centred * centred, axis=-1, keepdims=True)
    return centred * lax.rsqrt(spread + EPSILON) * norm_gain


def norm_back(skip_carry_tensor, norm_gain, upstream):
    _, pullback = jax.vjp(layer_norm, skip_carry_tensor, norm_gain)
    return pullback(upstream)


def exact_gelu(attention_contents):
    return jax.nn.gelu(attention_contents, approximate=False)


def spread_tokens(attention_contents):
    return lax.all_gather(attention_contents, "tp", axis=2, tiled=True)


def collect_tokens(attention_contents):
    return lax.psum_scatter(attention_contents, "tp", scatter_dimension=2, tiled=True)


def to_columns(attention_contents):
    return lax.all_to_all(attention_contents, "seq", split_axis=3, concat_axis=2, tiled=True)


def to_rows(attention_contents):
    return lax.all_to_all(attention_contents, "seq", split_axis=2, concat_axis=3, tiled=True)


def whole_probs(prob_low):
    return lax.all_gather(prob_low, "seq", axis=0, tiled=True)


def local(
    tokens,
    cotangent,
    lengths,
    column_mask,
    row_gain,
    row_qkv,
    row_out,
    col_gain,
    col_qkv,
    col_out,
    ffn_gain,
    ffn_up,
    ffn_down,
):
    aligns = tokens.shape[0]
    seq_dev = tokens.shape[1]
    cols = column_mask.shape[1]
    seqs = seq_dev * lax.axis_size("seq")
    query_rows = cols // lax.axis_size("seq")
    head_cols = row_qkv.shape[2]
    local_heads = head_cols // HEAD
    tied_scale = (HEAD * seqs) ** (-0.5)
    col_scale = HEAD ** (-0.5)
    position = jnp.arange(cols, dtype=jnp.int32)
    target_present_flags = (position[None, :] < lengths[:, None]) & (
        (column_mask == 1) | (position[None, :] == 0)
    )
    query_pos = lax.axis_index("seq") * query_rows + jnp.arange(query_rows, dtype=jnp.int32)
    source_present_flags = query_pos[:, None] < lengths[None, :]
    key_mask = target_present_flags[None, :, None, :]
    penalty_scale = (
        ENTROPY_WEIGHT * (aligns * seqs * cols) / (HEADS * jnp.sum(lengths).astype(jnp.float32))
    )
    residual = tokens.astype(jnp.float32)
    row_normed = spread_tokens(layer_norm(residual, row_gain).astype(jnp.bfloat16))
    row_proj = jnp.einsum(
        "asld,tdc->taslc", row_normed, row_qkv, preferred_element_type=jnp.float32
    ).astype(jnp.bfloat16)
    row_heads = row_proj.reshape(3, aligns, seq_dev, cols, local_heads, HEAD)
    row_query = row_heads[0]
    row_key = row_heads[1]
    row_value = row_heads[2]
    tied_logits = (
        lax.psum_scatter(
            jnp.einsum("asihe,asjhe->iahj", row_query, row_key, preferred_element_type=jnp.float32),
            "seq",
            scatter_dimension=0,
            tiled=True,
        )
        * tied_scale
    )
    masked = jnp.where(key_mask, tied_logits, NEGATIVE)
    row_top = jnp.max(masked, axis=-1, keepdims=True)
    row_powers = jnp.exp(masked - row_top)
    row_probs = row_powers / jnp.sum(row_powers, axis=-1, keepdims=True)
    prob_low = row_probs.astype(jnp.bfloat16)
    probs_full = whole_probs(prob_low)
    row_mixed = jnp.einsum(
        "iahj,asjhe->asihe", probs_full, row_value, preferred_element_type=jnp.float32
    )
    row_attended = row_mixed.astype(jnp.bfloat16).reshape(aligns, seq_dev, cols, head_cols)
    after_row = residual + collect_tokens(
        jnp.einsum("aslc,cd->asld", row_attended, row_out, preferred_element_type=jnp.float32)
    )
    col_normed = spread_tokens(layer_norm(after_row, col_gain).astype(jnp.bfloat16))
    col_proj = jnp.einsum(
        "asld,tdc->taslc", col_normed, col_qkv, preferred_element_type=jnp.float32
    ).astype(jnp.bfloat16)
    col_heads = to_columns(col_proj).reshape(3, aligns, seqs, query_rows, local_heads, HEAD)
    col_query = col_heads[0]
    col_key = col_heads[1]
    col_value = col_heads[2]
    col_scores = (
        jnp.einsum("asjhe,atjhe->ajhst", col_query, col_key, preferred_element_type=jnp.float32)
        * col_scale
    )
    column_upper_bound = jnp.max(col_scores, axis=-1, keepdims=True)
    col_powers = jnp.exp(col_scores - column_upper_bound)
    col_total = jnp.sum(col_powers, axis=-1, keepdims=True)
    col_lse = column_upper_bound + jnp.log(col_total)
    col_probs = (col_powers / col_total).astype(jnp.bfloat16)
    col_mixed = jnp.einsum(
        "ajhst,atjhe->asjhe", col_probs, col_value, preferred_element_type=jnp.float32
    ).astype(jnp.bfloat16)
    col_attended = to_rows(col_mixed.reshape(1, aligns, seqs, query_rows, head_cols))[0]
    after_col = after_row + collect_tokens(
        jnp.einsum("aslc,cd->asld", col_attended, col_out, preferred_element_type=jnp.float32)
    )
    ffn_local = layer_norm(after_col, ffn_gain).astype(jnp.bfloat16)
    ffn_normed = spread_tokens(ffn_local)
    ffn_pre = jnp.einsum("asld,df->aslf", ffn_normed, ffn_up, preferred_element_type=jnp.float32)
    ffn_hidden = exact_gelu(ffn_pre).astype(jnp.bfloat16)
    ffn_term = jnp.einsum("aslf,fd->asld", ffn_hidden, ffn_down, preferred_element_type=jnp.float32)
    block_out = after_col + collect_tokens(ffn_term)
    outputs = block_out.astype(jnp.bfloat16)
    outer_grad = cotangent.astype(jnp.float32)
    ffn_out_low = outer_grad.astype(jnp.bfloat16)
    ffn_out_in = spread_tokens(ffn_out_low)
    hidden_grad = jnp.einsum(
        "asld,fd->aslf", ffn_out_in, ffn_down, preferred_element_type=jnp.float32
    )
    _, gelu_pull = jax.vjp(exact_gelu, ffn_pre)
    pre_grad = gelu_pull(hidden_grad)[0].astype(jnp.bfloat16)
    down_grad = jnp.einsum(
        "aslf,asld->fd", ffn_hidden, ffn_out_in, preferred_element_type=jnp.float32
    )
    up_grad = jnp.einsum("asld,aslf->df", ffn_normed, pre_grad, preferred_element_type=jnp.float32)
    ffn_normed_grad = jnp.einsum(
        "aslf,df->asld", pre_grad, ffn_up, preferred_element_type=jnp.float32
    )
    ffn_normed_grad = collect_tokens(ffn_normed_grad)
    after_col_grad, ffn_gain_grad = norm_back(after_col, ffn_gain, ffn_normed_grad)
    middle_grad = outer_grad + after_col_grad
    col_out_in = spread_tokens(middle_grad.astype(jnp.bfloat16))
    col_out_grad = jnp.einsum(
        "aslc,asld->cd", col_attended, col_out_in, preferred_element_type=jnp.float32
    )
    col_mixed_grad = jnp.einsum(
        "asld,cd->aslc", col_out_in, col_out, preferred_element_type=jnp.float32
    ).astype(jnp.bfloat16)
    mixed_cols = to_columns(col_mixed_grad[None])[0].reshape(
        aligns, seqs, query_rows, local_heads, HEAD
    )
    col_again = jnp.exp(
        jnp.einsum("asjhe,atjhe->ajhst", col_query, col_key, preferred_element_type=jnp.float32)
        * col_scale
        - col_lse
    )
    col_value_grad = jnp.einsum(
        "ajhst,asjhe->atjhe",
        col_again.astype(jnp.bfloat16),
        mixed_cols,
        preferred_element_type=jnp.float32,
    )
    col_weight_grad = jnp.einsum(
        "asjhe,atjhe->ajhst", mixed_cols, col_value, preferred_element_type=jnp.float32
    )
    col_score_grad = (
        col_again * (col_weight_grad - jnp.sum(col_again * col_weight_grad, axis=-1, keepdims=True))
    ).astype(jnp.bfloat16)
    col_query_grad = (
        jnp.einsum(
            "ajhst,atjhe->asjhe", col_score_grad, col_key, preferred_element_type=jnp.float32
        )
        * col_scale
    )
    col_key_grad = (
        jnp.einsum(
            "ajhst,asjhe->atjhe", col_score_grad, col_query, preferred_element_type=jnp.float32
        )
        * col_scale
    )
    col_stack = jnp.stack([col_query_grad, col_key_grad, col_value_grad]).astype(jnp.bfloat16)
    col_proj_grad = to_rows(col_stack.reshape(3, aligns, seqs, query_rows, head_cols))
    col_qkv_grad = jnp.einsum(
        "asld,taslc->tdc", col_normed, col_proj_grad, preferred_element_type=jnp.float32
    )
    col_normed_grad = collect_tokens(
        jnp.einsum("taslc,tdc->asld", col_proj_grad, col_qkv, preferred_element_type=jnp.float32)
    )
    after_row_grad, col_gain_grad = norm_back(after_row, col_gain, col_normed_grad)
    inner_grad = middle_grad + after_row_grad
    row_out_in = spread_tokens(inner_grad.astype(jnp.bfloat16))
    row_out_grad = jnp.einsum(
        "aslc,asld->cd", row_attended, row_out_in, preferred_element_type=jnp.float32
    )
    row_mixed_grad = jnp.einsum(
        "asld,cd->aslc", row_out_in, row_out, preferred_element_type=jnp.float32
    ).astype(jnp.bfloat16)
    row_mixed_grad = row_mixed_grad.reshape(aligns, seq_dev, cols, local_heads, HEAD)
    prob_grad = lax.psum_scatter(
        jnp.einsum(
            "asihe,asjhe->iahj", row_mixed_grad, row_value, preferred_element_type=jnp.float32
        ),
        "seq",
        scatter_dimension=0,
        tiled=True,
    )
    prob_dot = jnp.sum(row_probs * prob_grad, axis=-1, keepdims=True)
    mean_logit = jnp.sum(jnp.where(key_mask, row_probs * masked, 0.0), axis=-1, keepdims=True)
    query_weight = jnp.where(source_present_flags[:, :, None, None], penalty_scale, 0.0)
    entropy_part = jnp.where(key_mask, row_probs * (masked - mean_logit), 0.0)
    logit_grad = (row_probs * (prob_grad - prob_dot) - query_weight * entropy_part).astype(
        jnp.bfloat16
    )
    logit_full = lax.all_gather(logit_grad, "seq", axis=0, tiled=True)
    probs_back = whole_probs(prob_low)
    row_query_grad = (
        jnp.einsum("iahj,asjhe->asihe", logit_full, row_key, preferred_element_type=jnp.float32)
        * tied_scale
    )
    row_key_grad = (
        jnp.einsum("iahj,asihe->asjhe", logit_full, row_query, preferred_element_type=jnp.float32)
        * tied_scale
    )
    row_value_grad = jnp.einsum(
        "iahj,asihe->asjhe", probs_back, row_mixed_grad, preferred_element_type=jnp.float32
    )
    row_stack = jnp.stack([row_query_grad, row_key_grad, row_value_grad]).astype(jnp.bfloat16)
    row_proj_grad = row_stack.reshape(3, aligns, seq_dev, cols, head_cols)
    row_qkv_grad = jnp.einsum(
        "asld,taslc->tdc", row_normed, row_proj_grad, preferred_element_type=jnp.float32
    )
    row_normed_grad = collect_tokens(
        jnp.einsum("taslc,tdc->asld", row_proj_grad, row_qkv, preferred_element_type=jnp.float32)
    )
    residual_grad, row_gain_grad = norm_back(residual, row_gain, row_normed_grad)
    input_grad = (inner_grad + residual_grad).astype(jnp.bfloat16)
    row_qkv_grad, row_out_grad, col_qkv_grad, col_out_grad, up_grad, down_grad = (
        lax.psum_scatter(row_qkv_grad, "seq", scatter_dimension=1, tiled=True),
        lax.psum_scatter(row_out_grad, "seq", scatter_dimension=1, tiled=True),
        lax.psum_scatter(col_qkv_grad, "seq", scatter_dimension=1, tiled=True),
        lax.psum_scatter(col_out_grad, "seq", scatter_dimension=1, tiled=True),
        lax.psum_scatter(up_grad, "seq", scatter_dimension=0, tiled=True),
        lax.psum_scatter(down_grad, "seq", scatter_dimension=1, tiled=True),
    )
    row_gain_grad, col_gain_grad, ffn_gain_grad = lax.psum(
        (row_gain_grad, col_gain_grad, ffn_gain_grad), ("seq", "tp")
    )
    return (
        outputs,
        input_grad,
        row_gain_grad,
        row_qkv_grad,
        row_out_grad,
        col_gain_grad,
        col_qkv_grad,
        col_out_grad,
        ffn_gain_grad,
        up_grad,
        down_grad,
    )


def solution(mesh):
    return jax.shard_map(
        local,
        mesh=mesh,
        in_specs=(
            P(None, "seq", "tp", None),
            P(None, "seq", "tp", None),
            P(),
            P(),
            P(),
            P(None, None, "tp"),
            P("tp", None),
            P(),
            P(None, None, "tp"),
            P("tp", None),
            P(),
            P(None, "tp"),
            P("tp", None),
        ),
        out_specs=(
            P(None, "seq", "tp", None),
            P(None, "seq", "tp", None),
            P(),
            P(None, "seq", "tp"),
            P("tp", "seq"),
            P(),
            P(None, "seq", "tp"),
            P("tp", "seq"),
            P(),
            P("seq", "tp"),
            P("tp", "seq"),
        ),
        check_vma=False,
    )
```

profile of v0, /device:TPU:0, one launch (start us, length us, event | category | flops | bytes accessed | tf_op | source)
XLA Modules:
  0.0 1358.9 jit_solution(14534029965693641955)
XLA Ops:
  11.8 39.9 %all-gather.9.cloned.1.call-done = bf16[1,1,1024,768]{3,2,1,0:T(8,128)(2,1)} async-done(((bf16[1,1,256,768]{3,2,1,0:T(8,128)(2,1)}), bf16[1,1,1024,768]{3,2,1,0:T(8,128)(2,1)}) %all-gather.9.cloned.1.call-update) | async-done | bytes 1572880 | tf_op jit(solution)/shard_map/all_gather | solution.py:32
  62.4 90.2 %reduce-scatter.23.cloned.1.call-done = f32[128,1,3,1024]{0,3,2,1:T(8,128)} async-done(((f32[1024,1,3,1024]{0,3,2,1:T(8,128)}), f32[128,1,3,1024]{0,3,2,1:T(8,128)}) %reduce-scatter.23.cloned.1.call-update) | async-done | bytes 1572880 | tf_op jit(solution)/shard_map/reduce_scatter | solution.py:95
  156.4 46.7 %all-gather.11.cloned.1.call-done = bf16[1024,1,3,1024]{0,3,2,1:T(8,128)(2,1)} async-done(((bf16[128,1,3,1024]{0,3,2,1:T(8,128)(2,1)}), bf16[1024,1,3,1024]{0,3,2,1:T(8,128)(2,1)}) %all-gather.11.cloned.1.call-update) | async-done | bytes 6291472 | tf_op jit(solution)/shard_map/all_gather | solution.py:48
  210.2 60.5 %reduce-scatter.25.cloned.1.call-done = f32[1,1,256,768]{3,2,1,0:T(8,128)} async-done(((f32[1,1,1024,768]{3,2,1,0:T(8,128)}), f32[1,1,256,768]{3,2,1,0:T(8,128)}) %reduce-scatter.25.cloned.1.call-update) | async-done | bytes 786448 | tf_op jit(solution)/shard_map/reduce_scatter | solution.py:36
  274.5 37.0 %all-gather.13.cloned.1.call-done = bf16[1,1,1024,768]{3,2,1,0:T(8,128)(2,1)} async-done(((bf16[1,1,256,768]{3,2,1,0:T(8,128)(2,1)}), bf16[1,1,1024,768]{3,2,1,0:T(8,128)(2,1)}) %all-gather.13.cloned.1.call-update) | async-done | bytes 1572880 | tf_op jit(solution)/shard_map/all_gather | solution.py:32
  319.6 30.4 %all_to_all.16 = bf16[3,1,1,1024,192]{4,0,2,1,3:T(4,128)(2,1)S(1)} all-to-all(bf16[3,1,1,1024,192]{4,0,2,1,3:T(4,128)(2,1)} %copy.102), channel_id=1, replica_groups=mesh['seq'=8,'tp'=4] {'seq'}, dimensions={3} | all-to-all | bytes 2359296 | tf_op jit(solution)/shard_map/all_to_all | solution.py:40
  384.5 11.8 all_to_all.17
  399.7 57.5 %reduce-scatter.27.cloned.1.call-done = f32[1,1,256,768]{3,2,1,0:T(8,128)} async-done(((f32[1,1,1024,768]{3,2,1,0:T(8,128)}), f32[1,1,256,768]{3,2,1,0:T(8,128)}) %reduce-scatter.27.cloned.1.call-update) | async-done | bytes 786448 | tf_op jit(solution)/shard_map/reduce_scatter | solution.py:36
  462.0 36.1 %all-gather.15.cloned.1.call-done = bf16[1,1,1024,768]{3,2,1,0:T(8,128)(2,1)} async-done(((bf16[1,1,256,768]{3,2,1,0:T(8,128)(2,1)}), bf16[1,1,1024,768]{3,2,1,0:T(8,128)(2,1)}) %all-gather.15.cloned.1.call-update) | async-done | bytes 1572880 | tf_op jit(solution)/shard_map/all_gather | solution.py:32
  508.8 26.8 %all-gather.17.cloned.1.call-done = bf16[1,1,1024,768]{3,2,1,0:T(8,128)(2,1)} async-done(((bf16[1,1,256,768]{3,2,1,0:T(8,128)(2,1)}), bf16[1,1,1024,768]{3,2,1,0:T(8,128)(2,1)}) %all-gather.17.cloned.1.call-update) | async-done | bytes 1572880 | tf_op jit(solution)/shard_map/all_gather | solution.py:32
  551.7 53.2 %reduce-scatter.31.cloned.1.call-done = f32[1,1,256,768]{3,2,1,0:T(8,128)} async-done(((f32[1,1,1024,768]{3,2,1,0:T(8,128)}), f32[1,1,256,768]{3,2,1,0:T(8,128)}) %reduce-scatter.31.cloned.1.call-update) | async-done | bytes 786448 | tf_op jit(solution)/shard_map/reduce_scatter | solution.py:36
  607.5 59.9 %reduce-scatter.29.cloned.1.call-done = f32[1,1,256,768]{3,2,1,0:T(8,128)} async-done(((f32[1,1,1024,768]{3,2,1,0:T(8,128)}), f32[1,1,256,768]{3,2,1,0:T(8,128)}) %reduce-scatter.29.cloned.1.call-update) | async-done | bytes 786448 | tf_op jit(solution)/shard_map/reduce_scatter | solution.py:36
  671.7 37.1 %all-gather.19.cloned.1.call-done = bf16[1,1,1024,768]{3,2,1,0:T(8,128)(2,1)} async-done(((bf16[1,1,256,768]{3,2,1,0:T(8,128)(2,1)}), bf16[1,1,1024,768]{3,2,1,0:T(8,128)(2,1)}) %all-gather.19.cloned.1.call-update) | async-done | bytes 1572880 | tf_op jit(solution)/shard_map/all_gather | solution.py:32
  754.0 19.3 %all_to_all.18 = bf16[3,1,8,128,192]{3,4,1,0,2:T(8,128)(2,1)S(1)} all-to-all(bf16[3,1,8,128,192]{3,4,1,0,2:T(8,128)(2,1)S(1)} %copy.124), channel_id=1, replica_groups=mesh['seq'=8,'tp'=4] {'seq'}, dimensions={2} | all-to-all | bytes 2359296 | tf_op jit(solution)/shard_map/all_to_all | solution.py:44
  782.9 57.6 %reduce-scatter.33.cloned.1.call-done = f32[1,1,256,768]{3,2,1,0:T(8,128)} async-done(((f32[1,1,1024,768]{3,2,1,0:T(8,128)}), f32[1,1,256,768]{3,2,1,0:T(8,128)}) %reduce-scatter.33.cloned.1.call-update) | async-done | bytes 786448 | tf_op jit(solution)/shard_map/reduce_scatter | solution.py:36
  846.3 37.0 %all-gather.21.cloned.1.call-done = bf16[1,1,1024,768]{3,2,1,0:T(8,128)(2,1)} async-done(((bf16[1,1,256,768]{3,2,1,0:T(8,128)(2,1)}), bf16[1,1,1024,768]{3,2,1,0:T(8,128)(2,1)}) %all-gather.21.cloned.1.call-update) | async-done | bytes 1572880 | tf_op jit(solution)/shard_map/all_gather | solution.py:32
  891.9 90.9 %reduce-scatter.35.cloned.1.call-done = f32[128,1,3,1024]{0,3,2,1:T(8,128)} async-done(((f32[1024,1,3,1024]{0,3,2,1:T(8,128)}), f32[128,1,3,1024]{0,3,2,1:T(8,128)}) %reduce-scatter.35.cloned.1.call-update) | async-done | bytes 1572880 | tf_op jit(solution)/shard_map/reduce_scatter | solution.py:222
  1011.0 22.5 %all-gather.23.cloned.1.call-done = bf16[1024,1,3,1024]{0,3,2,1:T(8,128)(2,1)} async-done(((bf16[128,1,3,1024]{0,3,2,1:T(8,128)(2,1)}), bf16[1024,1,3,1024]{0,3,2,1:T(8,128)(2,1)}) %all-gather.23.cloned.1.call-update) | async-done | bytes 6291472 | tf_op jit(solution)/shard_map/all_gather | solution.py:237
  1073.1 41.8 %reduce-scatter.47.cloned.1.call-done = f32[96,576]{1,0:T(8,128)} async-done(((f32[768,576]{1,0:T(8,128)}), f32[96,576]{1,0:T(8,128)}) %reduce-scatter.47.cloned.1.call-update) | async-done | bytes 221200
  1116.8 36.1 %reduce-scatter.45.cloned.1.call-done = f32[96,192]{1,0:T(8,128)} async-done(((f32[768,192]{1,0:T(8,128)}), f32[96,192]{1,0:T(8,128)}) %reduce-scatter.45.cloned.1.call-update) | async-done | bytes 73744
  1154.5 42.0 %reduce-scatter.43.cloned.1.call-done = f32[96,576]{1,0:T(8,128)} async-done(((f32[768,576]{1,0:T(8,128)}), f32[96,576]{1,0:T(8,128)}) %reduce-scatter.43.cloned.1.call-update) | async-done | bytes 221200
  1198.5 60.6 %reduce-scatter.37.cloned.1.call-done = f32[1,1,256,768]{3,2,1,0:T(8,128)} async-done(((f32[1,1,1024,768]{3,2,1,0:T(8,128)}), f32[1,1,256,768]{3,2,1,0:T(8,128)}) %reduce-scatter.37.cloned.1.call-update) | async-done | bytes 786448 | tf_op jit(solution)/shard_map/reduce_scatter | solution.py:36
  1261.6 40.3 %all-reduce = (f32[768]{0:T(1024)}, f32[768]{0:T(1024)}, f32[768]{0:T(1024)}) all-reduce(f32[768]{0:T(1024)S(1)} %get-tuple-element.72, f32[768]{0:T(1024)S(1)} %copy-done.57, f32[768]{0:T(1024)S(1)} %copy-done.56), channel_id=1, replica_groups=mesh['seq'=8,'tp'=4] {'seq','tp'}, use_global_device_ids=true, to_apply=%region_28.29 | all-reduce | flops 2304 | bytes 18432 | tf_op jit(solution)/shard_map/psum | solution.py:268
  1305.4 46.5 %reduce-scatter.39.cloned.1.call-done = f32[96,768]{1,0:T(8,128)} async-done(((f32[768,768]{1,0:T(8,128)}), f32[96,768]{1,0:T(8,128)}) %reduce-scatter.39.cloned.1.call-update) | async-done | bytes 294928 | tf_op jit(solution)/shard_map/reduce_scatter | solution.py:265
  (317 shorter events, 261.3 us)
Async XLA Ops:
  7.2 490.9 %copy-start = (bf16[768,768]{1,0:T(8,128)(2,1)S(1)}, bf16[768,768]{1,0:T(8,128)(2,1)}, u32[]{:S(2)}) copy-start(bf16[768,768]{1,0:T(8,128)(2,1)} %param.24) | copy-start | bytes 3538948
  7.2 44.5 %all-gather.9.cloned.1.call-start = ((), (), s32[]{:S(2)}) async-start(), calls=%async_computation.18 | async-start | bytes 1966080 | tf_op jit(solution)/shard_map/all_gather | solution.py:32
  11.8 140.8 %reduce-scatter.23.cloned.1.call-start = ((), (), s32[]{:S(2)}) async-start(), calls=%async_computation.19 | async-start | bytes 14155776 | tf_op jit(solution)/shard_map/reduce_scatter | solution.py:95
  61.6 141.4 %all-gather.11.cloned.1.call-start = ((), (), s32[]{:S(2)}) async-start(), calls=%async_computation.20 | async-start | bytes 7077888 | tf_op jit(solution)/shard_map/all_gather | solution.py:48
  156.3 114.4 %reduce-scatter.25.cloned.1.call-start = ((), (), s32[]{:S(2)}) async-start(), calls=%async_computation.21 | async-start | bytes 3932160 | tf_op jit(solution)/shard_map/reduce_scatter | solution.py:36
  210.2 101.4 %all-gather.13.cloned.1.call-start = ((), (), s32[]{:S(2)}) async-start(), calls=%async_computation.22 | async-start | bytes 1966080 | tf_op jit(solution)/shard_map/all_gather | solution.py:32
  274.4 182.8 %reduce-scatter.27.cloned.1.call-start = ((), (), s32[]{:S(2)}) async-start(), calls=%async_computation.23 | async-start | bytes 3932160 | tf_op jit(solution)/shard_map/reduce_scatter | solution.py:36
  399.7 98.4 %all-gather.15.cloned.1.call-start = ((), (), s32[]{:S(2)}) async-start(), calls=%async_computation.24 | async-start | bytes 1966080 | tf_op jit(solution)/shard_map/all_gather | solution.py:32
  461.0 74.6 %all-gather.17.cloned.1.call-start = ((), (), s32[]{:S(2)}) async-start(), calls=%async_computation.26 | async-start | bytes 1966080 | tf_op jit(solution)/shard_map/all_gather | solution.py:32
  461.8 143.1 %reduce-scatter.31.cloned.1.call-start = ((), (), s32[]{:S(2)}) async-start(), calls=%async_computation.27 | async-start | bytes 3932160 | tf_op jit(solution)/shard_map/reduce_scatter | solution.py:36
  545.5 121.9 %reduce-scatter.29.cloned.1.call-start = ((), (), s32[]{:S(2)}) async-start(), calls=%async_computation.25 | async-start | bytes 3932160 | tf_op jit(solution)/shard_map/reduce_scatter | solution.py:36
  551.2 157.5 %all-gather.19.cloned.1.call-start = ((), (), s32[]{:S(2)}) async-start(), calls=%async_computation.28 | async-start | bytes 1966080 | tf_op jit(solution)/shard_map/all_gather | solution.py:32
  719.7 12.0 all-to-all-start.2
  723.3 117.1 %reduce-scatter.33.cloned.1.call-start = ((), (), s32[]{:S(2)}) async-start(), calls=%async_computation.29 | async-start | bytes 3932160 | tf_op jit(solution)/shard_map/reduce_scatter | solution.py:36
  782.8 100.5 %all-gather.21.cloned.1.call-start = ((), (), s32[]{:S(2)}) async-start(), calls=%async_computation.30 | async-start | bytes 1966080 | tf_op jit(solution)/shard_map/all_gather | solution.py:32
  846.2 136.5 %reduce-scatter.35.cloned.1.call-start = ((), (), s32[]{:S(2)}) async-start(), calls=%async_computation.31 | async-start | bytes 14155776 | tf_op jit(solution)/shard_map/reduce_scatter | solution.py:222
  891.8 141.7 %all-gather.23.cloned.1.call-start = ((), (), s32[]{:S(2)}) async-start(), calls=%async_computation.32 | async-start | bytes 7077888 | tf_op jit(solution)/shard_map/all_gather | solution.py:237
  986.7 84.7 %reduce-scatter.49.cloned.1.call-start = ((), (), s32[]{:S(2)}) async-start(), calls=%async_computation.39 | async-start | bytes 884736
  989.9 125.0 %reduce-scatter.47.cloned.1.call-start = ((), (), s32[]{:S(2)}) async-start(), calls=%async_computation.38 | async-start | bytes 2211840
  1002.7 150.2 %reduce-scatter.45.cloned.1.call-start = ((), (), s32[]{:S(2)}) async-start(), calls=%async_computation.37 | async-start | bytes 884736
  1005.9 190.6 %reduce-scatter.43.cloned.1.call-start = ((), (), s32[]{:S(2)}) async-start(), calls=%async_computation.36 | async-start | bytes 2211840
  1048.4 210.7 %reduce-scatter.37.cloned.1.call-start = ((), (), s32[]{:S(2)}) async-start(), calls=%async_computation.33 | async-start | bytes 3932160 | tf_op jit(solution)/shard_map/reduce_scatter | solution.py:36
  1052.6 252.7 %reduce-scatter.41.cloned.1.call-start = ((), (), s32[]{:S(2)}) async-start(), calls=%async_computation.35 | async-start | bytes 2654208 | tf_op jit(solution)/shard_map/reduce_scatter | solution.py:266
  1058.3 293.6 %reduce-scatter.39.cloned.1.call-start = ((), (), s32[]{:S(2)}) async-start(), calls=%async_computation.34 | async-start | bytes 2654208 | tf_op jit(solution)/shard_map/reduce_scatter | solution.py:265
  (78 other events, 2582.3 us)
Sparse Core Ops, SparseCore 0:
  11.9 39.7 all-gather.8
  61.8 90.8 reduce-scatter.22
  156.4 46.5 all-gather.10
  210.3 60.3 reduce-scatter.24
  274.6 36.9 all-gather.12
  399.8 57.4 reduce-scatter.26
  461.1 36.9 all-gather.14
  499.7 35.8 all-gather.16
  545.6 59.2 reduce-scatter.30
  607.1 60.2 reduce-scatter.28
  671.8 36.9 all-gather.18
  783.0 57.4 reduce-scatter.32
  846.4 36.9 all-gather.20
  891.9 90.8 reduce-scatter.34
  986.8 46.5 all-gather.22
  1036.5 34.9 reduce-scatter.48
  1074.7 40.1 reduce-scatter.46
  1117.9 34.9 reduce-scatter.44
  1156.3 40.1 reduce-scatter.42
  1198.6 60.3 reduce-scatter.36
  1263.0 42.3 reduce-scatter.40
  1309.3 42.5 reduce-scatter.38
where the time goes:
time: 1370 us; the launch traced here: 1360 us
  waiting for transfers between devices  995 us (73%)
  matrix products  102 us (7%)
  blocking collectives  102 us (7%)
  local copies, waits for them, and re-layouts  94.6 us (7%)
  other arithmetic  43.8 us (3%)
  between operations  16.1 us (1%)
    reduce_scatter x6, waiting for transfers between devices, collect_tokens(): lax.psum_scatter(attention_contents, 'tp', scatter_dimension=2, tiled=True)  349 us
    all_gather x6, waiting for transfers between devices, spread_tokens(): return lax.all_gather(attention_contents, 'tp', axis=2, tiled=True)  214 us
    unnamed x26, waiting for transfers between devices  128 us
    reduce_scatter x1, waiting for transfers between devices, local(): lax.psum_scatter(jnp.einsum('asihe,asjhe->iahj', row_mixed_grad, row_valu...  90.9 us
    reduce_scatter x1, waiting for transfers between devices, local(): lax.psum_scatter(jnp.einsum('asihe,asjhe->iahj', row_query, row_key, pref...  90.2 us
    unnamed x175, local copies, waits for them, and re-layouts  50 us
    all_gather x1, waiting for transfers between devices, whole_probs(): return lax.all_gather(prob_low, 'seq', axis=0, tiled=True)  46.7 us
    reduce_scatter x1, waiting for transfers between devices, local(): lax.psum_scatter(up_grad, 'seq', scatter_dimension=0, tiled=True)  46.5 us
  transfers between devices with their start and end apart: 23, of which 23 were waited for; matrix products, arithmetic and copies ran while one was open for 6% of the time, Pallas kernels for 0%

commit v1 on v0

v1 whole, which is shorter than its diff:
```python
import functools

import jax
import jax.numpy as jnp
from jax import lax
from jax.experimental import pallas as pl
from jax.experimental.pallas import tpu as pltpu
from jax.sharding import Mesh
from jax.sharding import PartitionSpec as P

HEADS = 12
HEAD = 64
EPSILON = 1e-05
NEGATIVE = -1e30
ENTROPY_WEIGHT = 4.0

SEQ = ("c", "r")
BF = jnp.bfloat16
F32 = jnp.float32
VMEM_LIMIT = 60 * 1024 * 1024


def statistics(value):
    average = jnp.mean(value, axis=-1, keepdims=True)
    centred = value - average
    inverse = lax.rsqrt(jnp.mean(centred * centred, axis=-1, keepdims=True) + EPSILON)
    return centred * inverse, inverse


def layer_norm(value, gain):
    unit, _ = statistics(value)
    return unit * gain


def norm_back(value, gain, upstream):
    unit, inverse = statistics(value)
    scaled = upstream * gain
    back = inverse * (
        scaled
        - jnp.mean(scaled, axis=-1, keepdims=True)
        - unit * jnp.mean(scaled * unit, axis=-1, keepdims=True)
    )
    return back, jnp.sum(upstream * unit, axis=0, keepdims=True)


def gelu_parts(value):
    share = 0.5 * (1.0 + lax.erf(value * (0.5**0.5)))
    slope = share + value * jnp.exp(-0.5 * value * value) * 0.3989422804014327
    return value * share, slope


def mm(left, right):
    return lax.dot_general(left, right, (((1,), (0,)), ((), ())), preferred_element_type=F32)


def mm_nt(left, right):
    return lax.dot_general(left, right, (((1,), (1,)), ((), ())), preferred_element_type=F32)


def swap(value, axis, size, mask):
    return lax.ppermute(value, axis, [(i, i ^ mask) for i in range(size)])


def bits_of(size):
    return [1 << b for b in range(size.bit_length() - 1)]


def exchange(value, axis):
    return lax.all_to_all(value, axis, split_axis=0, concat_axis=0, tiled=True)


ANY = pl.BlockSpec(memory_space=pl.ANY)
VMEM = pl.BlockSpec(memory_space=pltpu.VMEM)
SMEM = pl.BlockSpec(memory_space=pltpu.SMEM)


def call(body, outs, *args, specs=None, scratch=(), flops=0, moved=0):
    inner = body.func if isinstance(body, functools.partial) else body
    cost = pl.CostEstimate(flops=int(flops), bytes_accessed=int(moved), transcendentals=0)
    return pl.pallas_call(
        body,
        out_shape=[jax.ShapeDtypeStruct(shape, kind) for shape, kind in outs],
        in_specs=[VMEM] * len(args) if specs is None else specs,
        out_specs=[VMEM] * len(outs),
        scratch_shapes=list(scratch),
        compiler_params=pltpu.CompilerParams(vmem_limit_bytes=VMEM_LIMIT),
        cost_estimate=cost if flops else None,
        name=inner.__name__,
    )(*args)


def fetch(me_ref, tp, shard, parts, store, sems):
    copies = [[pltpu.make_async_copy(shard, store.at[0], sems.at[0, 0])]]
    for k in range(1, tp):
        if len(parts) == 1:
            source = parts[0].at[me_ref[1] ^ k]
            copies.append([pltpu.make_async_copy(source, store.at[k], sems.at[k, 0])])
        else:
            copies.append(
                [
                    pltpu.make_async_copy(
                        part.at[k - 1], store.at[k, me_ref[0] ^ m], sems.at[k, m]
                    )
                    for m, part in enumerate(parts)
                ]
            )
    for group in copies:
        for copy in group:
            copy.start()

    def wait(k):
        for copy in copies[k]:
            copy.wait()

    return wait


def relative_rows(me_ref, order, turned, store):
    if order is None:
        return turned
    store[...] = turned
    rows = turned.shape[0] >> len(order)
    picked = []
    for m in range(1 << len(order)):
        mask = sum(((m >> (len(order) - 1 - i)) & 1) << bit for i, bit in enumerate(order))
        start = pl.multiple_of((me_ref[0] ^ mask) * rows, rows)
        picked.append(store[pl.ds(start, rows), :])
    return jnp.concatenate(picked, axis=0)


def store_rows(me_ref, order, refs, k, columns, value):
    if order is None:
        refs[0][me_ref[1] ^ k, :, columns] = value
        return
    half = value.shape[0] // 2
    for ref, part in zip(refs, (value[:half], value[half:])):
        ref[:, k, :, columns] = part.reshape(ref.shape[0], ref.shape[2], -1)


def project(dims, me_ref, *refs):
    slots, ranks, few, tp, heads = dims
    blocks, (gain, weight, normed, pieces) = refs[:tp], refs[tp:]
    features = heads * HEAD
    part = slots * few
    pieces[heads * ranks :] = jnp.zeros_like(pieces[heads * ranks :])
    for k in range(tp):
        z = me_ref[1] ^ k
        value = blocks[k][...].astype(F32).reshape(slots, ranks, few, -1)
        value = jnp.concatenate(
            [value[c, r] for r in range(ranks) for c in range(slots)], axis=0
        )
        low = layer_norm(value, gain[...]).astype(BF)
        normed[z] = low
        columns = pl.ds(pl.multiple_of(z * part, part), part)
        proj = mm_nt(weight[...], low).astype(BF)
        for c in range(heads):
            for r in range(ranks):
                for t in range(3):
                    rows = t * features + c * HEAD
                    piece = proj[rows : rows + HEAD, r * part : (r + 1) * part]
                    pieces[c * ranks + r, t, :, columns] = piece


def tied_softmax(own, other, key_ok, scale):
    depth = own.shape[0] * own.shape[2]
    turned = own[:, 0].reshape(depth, -1).T
    logits = jnp.concatenate(
        [mm(turned, pair[:, 1].reshape(depth, -1)) for pair in (own, other)], axis=1
    )
    ok = key_ok[...] > 0
    masked = jnp.where(ok, logits * scale, NEGATIVE)
    powers = jnp.exp(masked - jnp.max(masked, axis=-1, keepdims=True))
    return masked, powers * (1.0 / jnp.sum(powers, axis=-1, keepdims=True)), ok


def attend(scale, own, other, key_ok, mixed):
    _, probs, _ = tied_softmax(own, other, key_ok, scale)
    depth = own.shape[0] * own.shape[2]
    low = probs.astype(BF)
    half = low.shape[1] // 2
    total = mm_nt(low[:, :half], own[:, 2].reshape(depth, -1))
    total += mm_nt(low[:, half:], other[:, 2].reshape(depth, -1))
    mixed[...] = total.astype(BF).reshape(mixed.shape)


def attend_back(scale, own, other, key_ok, weight, mixed_grad, query_grad, kept, given):
    masked, probs, ok = tied_softmax(own, other, key_ok, scale)
    seqs = own.shape[0]
    depth = seqs * own.shape[2]
    low = probs.astype(BF)
    half = low.shape[1] // 2
    out_grad = mixed_grad[...].reshape(-1, depth)
    prob_grad = jnp.concatenate(
        [mm(out_grad, pair[:, 2].reshape(depth, -1)) for pair in (own, other)], axis=1
    )
    prob_dot = jnp.sum(probs * prob_grad, axis=-1, keepdims=True)
    mean_logit = jnp.sum(jnp.where(ok, probs * masked, 0.0), axis=-1, keepdims=True)
    entropy = jnp.where(ok, probs * (masked - mean_logit), 0.0)
    grad = (probs * (prob_grad - prob_dot) - weight[...] * entropy).astype(BF)
    total = mm_nt(own[:, 1].reshape(depth, -1), grad[:, :half])
    total += mm_nt(other[:, 1].reshape(depth, -1), grad[:, half:])
    query_grad[...] = (total * scale).astype(BF).reshape(query_grad.shape)
    turned = out_grad.T
    flat = own[:, 0].reshape(depth, -1)
    shape = (seqs, HEAD, half)
    given[:, 0] = (mm(flat, grad[:, half:]) * scale).astype(BF).reshape(shape)
    given[:, 1] = mm(turned, low[:, half:]).astype(BF).reshape(shape)
    kept[:, 0] = (mm(flat, grad[:, :half]) * scale).reshape(shape)
    kept[:, 1] = mm(turned, low[:, :half]).reshape(shape)


def column_probs(query, key, rule, scale):
    scores = jnp.where(rule, mm_nt(query, key) * scale, NEGATIVE)
    powers = jnp.exp(scores - jnp.max(scores, axis=-1, keepdims=True))
    return powers * (1.0 / jnp.sum(powers, axis=-1, keepdims=True))


def same_column(count, few):
    rows = lax.broadcasted_iota(jnp.int32, (count, count), 0)
    columns = lax.broadcasted_iota(jnp.int32, (count, count), 1)
    return (rows % few) == (columns % few)


def narrow(store, k, features):
    whole = store[k].reshape(-1, store.shape[3])
    return [whole[i * features : (i + 1) * features] for i in range(5)]


def columns_forward(dims, parts, me_ref, tokens, attended, gain, shard, *refs):
    few, tp, heads = dims
    parts, (after_row, normed, proj, mixed, after_col, store, sems) = refs[:parts], refs[parts:]
    wait = fetch(me_ref, tp, shard, parts, store, sems)
    features = heads * HEAD
    count = tokens.shape[0]
    total = tokens[...].astype(F32)

    update = jnp.zeros_like(total)
    for k in range(tp):
        wait(k)
        update += mm(attended[me_ref[1] ^ k], narrow(store, k, features)[0])
    total = total + update
    after_row[...] = total
    low = layer_norm(total, gain[...]).astype(BF)
    normed[...] = low
    rule = same_column(count, few)
    update = jnp.zeros_like(total)
    for k in range(tp):
        weights = narrow(store, k, features)
        for t in range(3):
            proj[t, k] = mm_nt(low, weights[2 + t]).astype(BF)
        for h in range(heads):
            at = slice(h * HEAD, (h + 1) * HEAD)
            probs = column_probs(proj[0, k, :, at], proj[1, k, :, at], rule, HEAD**-0.5)
            mixed[k, :, at] = mm(probs.astype(BF), proj[2, k, :, at]).astype(BF)
        update += mm(mixed[k], weights[1])
    after_col[...] = total + update


def columns_backward(dims, parts, order, me_ref, *refs):
    few, tp, heads = dims
    middle, after_row, normed, proj, mixed, attended, gain, shard = refs[:8]
    parts, refs = refs[8 : 8 + parts], refs[8 + parts :]
    inner, inner_low, row_mixed, gain_grad = refs[:4]
    grads, (col_grad, rows, store, sems) = refs[4:-4], refs[-4:]
    wait = fetch(me_ref, tp, shard, parts, store, sems)
    features = heads * HEAD
    count = middle.shape[0]
    middle_low = middle[...].astype(BF)
    turned = relative_rows(me_ref, order, middle_low.T, rows)
    normed_turned = relative_rows(me_ref, order, normed[...].T, rows)
    rule = same_column(count, few)
    upstream = jnp.zeros(middle.shape, F32)
    for k in range(tp):
        wait(k)
        weights = narrow(store, k, features)
        mixed_grad = mm_nt(middle_low, weights[1]).astype(BF)
        for h in range(heads):
            at = slice(h * HEAD, (h + 1) * HEAD)
            query, key, value = proj[0, k, :, at], proj[1, k, :, at], proj[2, k, :, at]
            probs = column_probs(query, key, rule, HEAD**-0.5)
            out_grad = mixed_grad[:, at]
            prob_grad = mm_nt(out_grad, value)
            score = probs * (prob_grad - jnp.sum(probs * prob_grad, axis=-1, keepdims=True))
            score = score.astype(BF)
            col_grad[0, :, at] = (mm(score, key) * HEAD**-0.5).astype(BF)
            col_grad[1, :, at] = (mm(score.T, query) * HEAD**-0.5).astype(BF)
            col_grad[2, :, at] = mm(probs.astype(BF).T, out_grad).astype(BF)
        pieces = []
        for t in range(3):
            upstream += mm(col_grad[t], weights[2 + t])
            pieces.append(mm(normed_turned, col_grad[t]).astype(BF))
        pieces.append(mm(turned, mixed[k]).astype(BF))
        store_rows(
            me_ref, order, grads, k, slice(0, 4 * features), jnp.concatenate(pieces, axis=1)
        )
    back, gain_grad[...] = norm_back(after_row[...], gain[...], upstream)
    total = middle[...] + back
    inner[...] = total
    low = total.astype(BF)
    inner_low[...] = low
    turned = relative_rows(me_ref, order, low.T, rows)
    for k in range(tp):
        z = me_ref[1] ^ k
        value = mm(turned, attended[z]).astype(BF)
        store_rows(me_ref, order, grads, k, slice(4 * features, 5 * features), value)
        row_mixed[z] = mm_nt(low, narrow(store, k, features)[0]).astype(BF)


def feed_forward(tp, parts, orders, me_ref, after_col, cotangent, gain, up_shard, down_shard, *refs):
    parts, refs = refs[:parts], refs[parts:]
    outputs, middle, gain_grad = refs[:3]
    grads, (rows, store, sems) = refs[3:-3], refs[-3:]
    count = len(grads) // 2
    half = store.shape[1] // 2
    own_up = pltpu.make_async_copy(up_shard, store.at[0, :half], sems.at[0, 0])
    own_down = pltpu.make_async_copy(down_shard, store.at[0, half:], sems.at[0, 1])
    copies = [[own_up, own_down]]
    for k in range(1, tp):
        if len(parts) == 1:
            source = parts[0].at[me_ref[1] ^ k]
            copies.append([pltpu.make_async_copy(source, store.at[k], sems.at[k, 0])])
        else:
            copies.append(
                [
                    pltpu.make_async_copy(
                        part.at[k - 1], store.at[k, me_ref[0] ^ m], sems.at[k, m]
                    )
                    for m, part in enumerate(parts)
                ]
            )
    for group in copies:
        for copy in group:
            copy.start()
    value = after_col[...]
    low = layer_norm(value, gain[...]).astype(BF)
    given = cotangent[...]
    low_turned = relative_rows(me_ref, orders[0], low.T, rows)
    given_turned = relative_rows(me_ref, orders[1], given.T, rows)
    result = value
    upstream = jnp.zeros_like(value)
    for k in range(tp):
        for copy in copies[k]:
            copy.wait()
        up = store[k, :half].reshape(-1, store.shape[3])
        down = store[k, half:].reshape(-1, store.shape[3])
        hidden, slope = gelu_parts(mm(low, up))
        hidden = hidden.astype(BF)
        result += mm(hidden, down)
        pre_grad = (mm_nt(given, down) * slope).astype(BF)
        upstream += mm_nt(pre_grad, up)
        everything = slice(0, up.shape[1])
        value_up = mm(low_turned, pre_grad).astype(BF)
        store_rows(me_ref, orders[0], grads[:count], k, everything, value_up)
        value_down = mm(given_turned, hidden).astype(BF)
        store_rows(me_ref, orders[1], grads[count:], k, everything, value_down)
    outputs[...] = result.astype(BF)
    back, gain_grad[...] = norm_back(value, gain[...], upstream)
    middle[...] = given.astype(F32) + back


def gather_grads(dims, order, me_ref, pieces_in, normed, gain, weight, *outs):
    slots, ranks, few, tp, heads = dims
    features = heads * HEAD
    part = slots * few
    pieces, (kept, sent, gain_grad, rows) = outs[:tp], outs[tp:]
    total = jnp.zeros((3 * features, normed.shape[2]), F32)
    for k in range(tp):
        z = me_ref[1] ^ k
        columns = pl.ds(pl.multiple_of(z * part, part), part)
        for c in range(heads):
            for r in range(ranks):
                for t in range(3):
                    piece = pieces_in[c * ranks + r, t, :, columns]
                    at = t * features + c * HEAD
                    pieces[k][at : at + HEAD, r * part : (r + 1) * part] = piece
        total += mm(pieces[k][...], normed[z])
    gain_grad[...] = (
        jnp.sum(total * weight[...].astype(F32), axis=0, keepdims=True) / gain[...]
    )
    turned = relative_rows(me_ref, order, total.T.astype(BF), rows)
    half = turned.shape[0] // 2
    kept[...] = turned[:half].reshape(kept.shape)
    sent[...] = turned[half:].reshape(sent.shape)


def finish(dims, parts, me_ref, *refs):
    slots, ranks, few, tp, heads = dims
    features = heads * HEAD
    pieces, refs = refs[:tp], refs[tp:]
    tokens, gain, inner, shard = refs[:4]
    parts, (result, store, sems) = refs[4 : 4 + parts], refs[4 + parts :]
    wait = fetch(me_ref, tp, shard, parts, store, sems)
    upstream = jnp.zeros(inner.shape, F32)
    for k in range(tp):
        wait(k)
        whole = store[k].reshape(-1, store.shape[3])[: 3 * features]
        upstream += mm(pieces[k][...].T, whole)
    upstream = upstream.reshape(ranks, slots, few, -1)
    upstream = jnp.concatenate(
        [upstream[r, c] for c in range(slots) for r in range(ranks)], axis=0
    )
    back, _ = norm_back(tokens[...].astype(F32), gain[...], upstream)
    result[...] = (inner[...].astype(F32) + back).astype(BF)


def after(value, *others):
    return lax.optimization_barrier((value,) + others)[0]


def add(left, right):
    return (left.astype(F32) + right.astype(F32)).astype(BF)


def local(
    tokens,
    cotangent,
    lengths,
    column_mask,
    row_gain,
    row_qkv,
    row_out,
    col_gain,
    col_qkv,
    col_out,
    ffn_gain,
    ffn_up,
    ffn_down,
):
    slots, ranks, tp = lax.axis_size("c"), lax.axis_size("r"), lax.axis_size("tp")
    seqs = slots * ranks
    block, width = tokens.shape[2], tokens.shape[3]
    cols = column_mask.shape[1]
    few = block // seqs
    part = slots * few
    features = row_qkv.shape[2]
    heads = features // HEAD
    hidden = ffn_up.shape[1]
    queries = tp * part
    count = seqs * few
    tied_scale = (HEAD * seqs) ** (-0.5)
    my_seq, my_rank, my_z = lax.axis_index(SEQ), lax.axis_index("r"), lax.axis_index("tp")
    me_ref = jnp.stack([my_seq, my_z]).astype(jnp.int32)
    dims = (slots, ranks, few, tp, heads)
    fast = seqs == 8 and ranks == 2
    row_gain, col_gain, ffn_gain = row_gain[None], col_gain[None], ffn_gain[None]

    penalty_scale = ENTROPY_WEIGHT * (seqs * cols) / (HEADS * jnp.sum(lengths).astype(F32))
    position = jnp.arange(cols, dtype=jnp.int32).reshape(tp, slots, ranks, few)
    position = position.transpose(2, 0, 1, 3)
    flag = column_mask.reshape(tp, slots, ranks, few).transpose(2, 0, 1, 3)
    valid = (position < lengths[0]) & ((flag == 1) | (position == 0))
    valid = valid.astype(F32).reshape(ranks, queries)
    key_ok = jnp.concatenate(
        [lax.dynamic_index_in_dim(valid, my_rank ^ k, 0) for k in range(ranks)], axis=1
    )
    query_position = lax.dynamic_index_in_dim(position.reshape(ranks, queries), my_rank, 0)
    query_weight = jnp.where(query_position < lengths[0], penalty_scale, 0.0).reshape(queries, 1)

    own = tokens[0, 0]
    blocks = [own] + [swap(own, "tp", tp, k) for k in range(1, tp)]
    residual = exchange(own.reshape(seqs, few, width), SEQ).reshape(count, width)
    given = exchange(cotangent[0, 0].reshape(seqs, few, width), SEQ).reshape(count, width)

    row_weight = row_qkv.transpose(0, 2, 1).reshape(3 * features, width)
    shard_a = jnp.concatenate(
        [row_out, col_out, col_qkv.transpose(0, 2, 1).reshape(3 * features, width)]
    )

    def cut(shard, least):
        rows = shard.shape[0]
        rows += -rows % (seqs * least)
        shard = jnp.pad(shard, ((0, rows - shard.shape[0]), (0, 0)))
        return shard.reshape(seqs, rows // seqs, width)

    shard_a = cut(shard_a, 16 if fast else 1)
    shard_c = cut(row_weight, 16 if fast else 1)
    shard_b = cut(jnp.concatenate([ffn_up, ffn_down]), 1)

    def mine(shard):
        return lax.dynamic_index_in_dim(shard, my_seq, 0, keepdims=False)

    def along_tp(piece):
        return jnp.stack([swap(piece, "tp", tp, k) for k in range(1, tp)])

    def along_seq(held, masks, gate=None):
        first = swap(held, "c", slots, masks[0])
        second = [swap(p, "c", slots, masks[1]) for p in (held, first)]
        by_slot = {0: held, masks[0]: first, masks[1]: second[0], masks[0] ^ masks[1]: second[1]}
        by_slot = [by_slot[c] for c in range(4)]
        return [p for q in by_slot for p in (q, swap(q, "r", ranks, 1))]

    if fast:
        piece_a = after(mine(shard_a), *blocks[1:])
        near_a = along_tp(piece_a)
        near_b = along_tp(after(mine(shard_b), near_a))
        parts_a = along_seq(near_a, (1, 2))
        parts_b = along_seq(near_b, (2, 1))
        near_c = along_tp(after(mine(shard_c), *parts_b))
        parts_c = along_seq(near_c, (1, 2))
        blocks[1] = after(blocks[1], residual, given)
    else:

        def everywhere(shard):
            rows = shard.shape[0] * shard.shape[1]
            whole = lax.all_gather(mine(shard), ("tp",) + SEQ, axis=0)
            return [whole.reshape(tp, 8, rows // 8, width)]

        parts_a, parts_b, parts_c = everywhere(shard_a), everywhere(shard_b), everywhere(shard_c)
        shard_a = shard_a.reshape(8, -1, width)
        shard_c = shard_c.reshape(8, -1, width)
    up_own = ffn_up.reshape(4, -1, width)
    down_own = ffn_down.reshape(4, -1, width)
    store_a = pltpu.VMEM((tp,) + shard_a.shape, BF)
    store_b = pltpu.VMEM((tp, 8, shard_b.shape[0] * shard_b.shape[1] // 8, width), BF)
    store_c = pltpu.VMEM((tp,) + shard_c.shape, BF)
    sems = pltpu.SemaphoreType.DMA((tp, 8))

    if fast:
        normed, pieces = call(
            functools.partial(project, dims),
            [((tp, block, width), BF), ((seqs, 3, HEAD, queries), BF)],
            me_ref,
            *blocks,
            row_gain,
            row_weight,
            specs=[SMEM] + [VMEM] * (tp + 2),
            flops=2 * cols * width * 3 * features,
            moved=8 << 20,
        )
    else:
        order = jnp.stack(blocks)[my_z ^ jnp.arange(tp)]
        order = order.reshape(tp, slots, ranks, few, width).transpose(0, 2, 1, 3, 4)
        normed = layer_norm(order.astype(F32), row_gain).astype(BF).reshape(tp, block, width)
        pieces = jnp.einsum("fd,zld->fzl", row_weight, normed, preferred_element_type=F32)
        pieces = pieces.astype(BF).reshape(3, heads, HEAD, tp, ranks, part)
        pieces = pieces.transpose(1, 4, 0, 2, 3, 5).reshape(heads, ranks, 3, HEAD, queries)
        pieces = jnp.pad(pieces, ((0, slots - heads),) + ((0, 0),) * 4)
        pieces = pieces.reshape(seqs, 3, HEAD, queries)
    pieces = exchange(pieces, SEQ)
    mixed_shape = (tp * slots, few, seqs * HEAD)
    if fast:
        others = swap(pieces, "r", ranks, 1)
        (mixed,) = call(
            functools.partial(attend, tied_scale),
            [(mixed_shape, BF)],
            pieces,
            others,
            key_ok,
            flops=4 * cols * queries * seqs * HEAD,
            moved=8 << 20,
        )
    else:
        pairs = lax.all_gather(pieces[:, 1:], "r", axis=0)
        pairs = pairs.transpose(2, 1, 3, 0, 4).reshape(2, seqs * HEAD, cols)
        key, value = pairs[0], pairs[1]
        query = pieces[:, 0].reshape(seqs * HEAD, queries)
        key_ok = valid.reshape(1, cols)
        logits = jnp.einsum("ki,kj->ij", query, key, preferred_element_type=F32) * tied_scale
        masked = jnp.where(key_ok > 0, logits, NEGATIVE)
        powers = jnp.exp(masked - jnp.max(masked, axis=-1, keepdims=True))
        probs = powers / jnp.sum(powers, axis=-1, keepdims=True)
        mixed = jnp.einsum("ij,kj->ik", probs.astype(BF), value, preferred_element_type=F32)
        mixed = mixed.astype(BF).reshape(mixed_shape)
    mixed = exchange(mixed, ("tp", "c"))
    attended = (
        mixed.reshape(tp, slots, few, seqs, HEAD)[:, :heads]
        .transpose(0, 3, 2, 1, 4)
        .reshape(tp, count, features)
    )

    flat = (count, width)
    shards = (tp, count, features)
    n_parts = len(parts_a)
    after_row, col_normed, col_proj, col_mixed, after_col = call(
        functools.partial(columns_forward, (few, tp, heads), n_parts),
        [(flat, F32), (flat, BF), ((3,) + shards, BF), (shards, BF), (flat, F32)],
        me_ref,
        residual,
        attended,
        col_gain,
        shard_a,
        *parts_a,
        specs=[SMEM] + [VMEM] * 3 + [ANY] * (1 + n_parts),
        scratch=[store_a, sems],
        flops=2 * count * width * width * 5,
        moved=20 << 20,
    )
    if fast:
        grad_kinds = [((4, tp, width // seqs, hidden), BF)] * 4
        small_kinds = [((4, tp, width // seqs, 5 * features), BF)] * 2
        orders = ((0, 2, 1), (0, 1, 2))
    else:
        grad_kinds = [((tp, width, hidden), BF)] * 2
        small_kinds = [((tp, width, 5 * features), BF)]
        orders = (None, None)
    turned_rows = pltpu.VMEM((width, count), BF)
    outputs, middle, ffn_gain_grad, *wide_grads = call(
        functools.partial(feed_forward, tp, n_parts, orders),
        [(flat, BF), (flat, F32), ((1, width), F32)] + grad_kinds,
        me_ref,
        after_col,
        given,
        ffn_gain,
        up_own,
        down_own,
        *parts_b,
        specs=[SMEM] + [VMEM] * 3 + [ANY] * (2 + n_parts),
        scratch=[turned_rows, store_b, sems],
        flops=2 * count * width * hidden * tp * 6,
        moved=30 << 20,
    )
    outputs = exchange(outputs.reshape(seqs, few, width), SEQ).reshape(block, width)
    inner, inner_low, row_mixed, col_gain_grad, *small_grads = call(
        functools.partial(columns_backward, (few, tp, heads), n_parts, orders[1]),
        [(flat, F32), (flat, BF), (shards, BF), ((1, width), F32)] + small_kinds,
        me_ref,
        middle,
        after_row,
        col_normed,
        col_proj,
        col_mixed,
        attended,
        col_gain,
        shard_a,
        *parts_a,
        specs=[SMEM] + [VMEM] * 7 + [ANY] * (1 + n_parts),
        scratch=[pltpu.VMEM((3, count, features), BF), turned_rows, store_a, sems],
        flops=2 * count * width * width * 10,
        moved=30 << 20,
    )

    def first(kept, sent):
        return add(kept, swap(sent, "r", ranks, 1))

    def second(held, mask):
        half = held.shape[0] // 2
        return add(held[:half], swap(held[half:], "c", slots, mask))

    def last(held):
        total = held[0].astype(F32)
        for k in range(1, tp):
            total = total + swap(held[k], "tp", tp, k).astype(F32)
        return total

    def all_at_once(grad):
        grad = lax.psum_scatter(grad, SEQ, scatter_dimension=1, tiled=True)
        return lax.psum_scatter(grad, "tp", scatter_dimension=0, tiled=True)[0].astype(F32)

    row_mixed = row_mixed.reshape(tp, seqs, few, heads, HEAD).transpose(0, 3, 2, 1, 4)
    row_mixed = jnp.pad(row_mixed, ((0, 0), (0, slots - heads)) + ((0, 0),) * 3)
    row_mixed = exchange(row_mixed.reshape(mixed_shape), ("tp", "c"))
    inner_home = exchange(inner_low.reshape(seqs, few, width), SEQ).reshape(block, width)
    if fast:
        up_sum, down_sum = first(*wide_grads[:2]), first(*wide_grads[2:])
        row_mixed = after(row_mixed, up_sum, down_sum)
        query_grad, kept, sent = call(
            functools.partial(attend_back, tied_scale),
            [
                ((seqs, HEAD, queries), BF),
                ((seqs, 2, HEAD, queries), F32),
                ((seqs, 2, HEAD, queries), BF),
            ],
            pieces,
            others,
            key_ok,
            query_weight,
            row_mixed,
            flops=10 * cols * queries * seqs * HEAD,
            moved=16 << 20,
        )
        pair_grad = (kept + swap(sent, "r", ranks, 1).astype(F32)).astype(BF)
    else:
        out_grad = row_mixed.reshape(queries, seqs * HEAD)
        prob_grad = jnp.einsum("ik,kj->ij", out_grad, value, preferred_element_type=F32)
        prob_dot = jnp.sum(probs * prob_grad, axis=-1, keepdims=True)
        mean_logit = jnp.sum(
            jnp.where(key_ok > 0, probs * masked, 0.0), axis=-1, keepdims=True
        )
        entropy = jnp.where(key_ok > 0, probs * (masked - mean_logit), 0.0)
        grad = (probs * (prob_grad - prob_dot) - query_weight * entropy).astype(BF)
        total = jnp.einsum("ij,kj->ki", grad, key, preferred_element_type=F32)
        query_grad = (total * tied_scale).astype(BF).reshape(seqs, HEAD, queries)
        key_grad = jnp.einsum("ki,ij->kj", query, grad, preferred_element_type=F32)
        value_grad = jnp.einsum(
            "ik,ij->kj", out_grad, probs.astype(BF), preferred_element_type=F32
        )
        both = jnp.stack([(key_grad * tied_scale).astype(BF), value_grad.astype(BF)])
        both = both.reshape(2, seqs, HEAD, ranks, queries).transpose(3, 1, 0, 2, 4)
        pair_grad = lax.psum_scatter(both, "r", scatter_dimension=0, tiled=False)
    row_grad = exchange(jnp.concatenate([query_grad[:, None], pair_grad], axis=1), SEQ)
    if fast:
        up_sum, down_sum = second(up_sum, 2), second(down_sum, 1)
        small_sum = first(*small_grads)
        row_grad = after(row_grad, up_sum, down_sum, small_sum)
        *pieces, kept, sent, row_gain_grad = call(
            functools.partial(gather_grads, dims, (0, 2, 1)),
            [((3 * features, block), BF)] * tp
            + [((4, width // seqs, 3 * features), BF)] * 2
            + [((1, width), F32)],
            me_ref,
            row_grad,
            normed,
            row_gain,
            row_weight,
            specs=[SMEM] + [VMEM] * 4,
            scratch=[pltpu.VMEM((width, 3 * features), BF)],
            flops=2 * cols * width * 3 * features,
            moved=8 << 20,
        )
    else:
        both = row_grad.reshape(slots, ranks, 3, HEAD, tp, part)[:heads]
        both = both.transpose(4, 2, 0, 3, 1, 5).reshape(tp, 3 * features, block)
        row_grad = jnp.einsum("zld,zfl->df", normed, both, preferred_element_type=F32)
        row_gain_grad = (
            jnp.sum(row_grad.T * row_weight.astype(F32), axis=0, keepdims=True) / row_gain
        )
        pieces = [both[my_z ^ k] for k in range(tp)]
    pieces = [pieces[0]] + [swap(pieces[k], "tp", tp, k) for k in range(1, tp)]
    gains = jnp.concatenate([row_gain_grad, col_gain_grad, ffn_gain_grad], axis=0)
    for axis, size in (("r", ranks), ("c", slots), ("tp", tp)):
        for k in bits_of(size):
            gains = gains + swap(gains, axis, size, k)
    if fast:
        up_sum, down_sum = second(up_sum, 1)[0], second(down_sum, 2)[0]
        small_sum = second(small_sum, 1)
        row_grad = first(kept, sent)
        pieces[1] = after(pieces[1], up_sum, down_sum, small_sum, row_grad)
    (input_grad,) = call(
        functools.partial(finish, dims, n_parts),
        [((block, width), BF)],
        me_ref,
        *pieces,
        own,
        row_gain,
        inner_home,
        shard_c,
        *parts_c,
        specs=[SMEM] + [VMEM] * (tp + 3) + [ANY] * (1 + n_parts),
        scratch=[store_c, sems],
        flops=2 * block * width * width * 3,
        moved=8 << 20,
    )
    if fast:
        small_sum = second(small_sum, 2)[0]
        row_grad = second(row_grad, 2)
        row_grad = second(row_grad, 1)[0].astype(F32)
        up_grad, down_grad, small = last(up_sum), last(down_sum), last(small_sum)
    else:
        row_grad = lax.psum_scatter(row_grad, SEQ, scatter_dimension=0, tiled=True)
        up_grad, down_grad = all_at_once(wide_grads[0]), all_at_once(wide_grads[1])
        small = all_at_once(small_grads[0])

    def thirds(value):
        return value.reshape(width // seqs, 3, features).transpose(1, 0, 2)

    return (
        outputs[None, None],
        input_grad[None, None],
        gains[0],
        thirds(row_grad),
        small[:, 4 * features :].T,
        gains[1],
        thirds(small[:, : 3 * features]),
        small[:, 3 * features : 4 * features].T,
        gains[2],
        up_grad,
        down_grad.T,
    )


def solution(mesh):
    seqs, tp = mesh.shape["seq"], mesh.shape["tp"]
    heads = HEADS // tp
    slots = 1 << (heads - 1).bit_length()
    split = Mesh(mesh.devices.reshape(slots, seqs // slots, tp), ("c", "r", "tp"))
    return jax.shard_map(
        local,
        mesh=split,
        in_specs=(
            P(None, SEQ, "tp", None),
            P(None, SEQ, "tp", None),
            P(),
            P(),
            P(),
            P(None, None, "tp"),
            P("tp", None),
            P(),
            P(None, None, "tp"),
            P("tp", None),
            P(),
            P(None, "tp"),
            P("tp", None),
        ),
        out_specs=(
            P(None, SEQ, "tp", None),
            P(None, SEQ, "tp", None),
            P(),
            P(None, SEQ, "tp"),
            P("tp", SEQ),
            P(),
            P(None, SEQ, "tp"),
            P("tp", SEQ),
            P(),
            P(SEQ, "tp"),
            P("tp", SEQ),
        ),
        check_vma=False,
    )
```

time: 1370 us -> 504 us (0.37)
  waiting for transfers between devices: 995 us -> 256 us
  matrix products: 102 us -> 0 us
  blocking collectives: 102 us -> 0 us
  starting transfers between devices: 5.4 us -> 98.3 us
  Pallas kernels: 0 us -> 74.5 us
  local copies, waits for them, and re-layouts: 94.6 us -> 34.5 us
  other arithmetic: 43.8 us -> 30 us
    reduce_scatter x10 -> x0, waiting for transfers between devices: 577 us -> none  [the longest x6 349 us: collect_tokens(): lax.psum_scatter(attention_contents, 'tp', scatter_dimension=2, tiled=True)]
    all_gather x8 -> x0, waiting for transfers between devices: 283 us -> none  [the longest x6 214 us: spread_tokens(): return lax.all_gather(attention_contents, 'tp', axis=2, tiled=True)]
    ppermute x0 -> x64, waiting for transfers between devices: none -> 238 us  [swap(): return lax.ppermute(value, axis, [(i, i ^ mask) for i in range(size)])]
    unnamed x26 -> x0, waiting for transfers between devices: 128 us -> none
    dot_general x26 -> x0, matrix products: 92.1 us -> none  [the longest x1 10.7 us: local(): jnp.einsum('asld,df->aslf', ffn_normed, ffn_up, preferred_element_type=jn...]
    pallas_call x0 -> x8, Pallas kernels: none -> 74.5 us  [call(): pl.pallas_call(body, out_shape=[jax.ShapeDtypeStruct(shape, kind) for sha...]
    ppermute x0 -> x64, starting transfers between devices: none -> 66.2 us  [swap(): return lax.ppermute(value, axis, [(i, i ^ mask) for i in range(size)])]
    all_to_all x3 -> x0, blocking collectives: 61.5 us -> none  [the longest x2 31.1 us: to_rows(): lax.all_to_all(attention_contents, 'seq', split_axis=2, concat_axis=3, ti...]
  transfers between devices with their start and end apart: 23 -> 72, of which waited for: 23 -> 26; matrix products, arithmetic and copies ran while one was open for 6% -> 11% of each run, Pallas kernels for 0% -> 11%
where the time goes in v1:
time: 504 us; the launch traced here: 496 us
  waiting for transfers between devices  256 us (51%)
  starting transfers between devices  98.3 us (20%)
  Pallas kernels  74.5 us (15%)
  local copies, waits for them, and re-layouts  34.5 us (7%)
  other arithmetic  30 us (6%)
    ppermute x64, waiting for transfers between devices, swap(): return lax.ppermute(value, axis, [(i, i ^ mask) for i in range(size)])  238 us
    pallas_call x8, Pallas kernels, call(): pl.pallas_call(body, out_shape=[jax.ShapeDtypeStruct(shape, kind) for sha...  74.5 us
    ppermute x64, starting transfers between devices, swap(): return lax.ppermute(value, axis, [(i, i ^ mask) for i in range(size)])  66.2 us
    all_to_all x8, starting transfers between devices, exchange(): return lax.all_to_all(value, axis, split_axis=0, concat_axis=0, tiled=True)  32.1 us
    all_to_all x8, waiting for transfers between devices, exchange(): return lax.all_to_all(value, axis, split_axis=0, concat_axis=0, tiled=True)  18.6 us
    convert_element_type x11, other arithmetic, add(): return (left.astype(F32) + right.astype(F32)).astype(BF)  16.8 us
    unnamed x105, local copies, waits for them, and re-layouts  14.8 us
  transfers between devices with their start and end apart: 72, of which 26 were waited for; matrix products, arithmetic and copies ran while one was open for 11% of the time, Pallas kernels for 11%

profile of v1, /device:TPU:0, one launch (start us, length us, event | category | flops | bytes accessed | tf_op | source)
XLA Modules:
  0.0 496.2 jit_solution(13997703572067910248)
XLA Ops:
  19.5 6.4 %all-to-all-done = bf16[8,32,768]{2,1,0:T(8,128)(2,1)S(1)} async-done(((bf16[8,32,768]{2,1,0:T(8,128)(2,1)}), bf16[8,32,768]{2,1,0:T(8,128)(2,1)S(1)}, u32[]{:S(2)}, u32[]{:S(2)}) %all-to-all-start) | async-done | bytes 393248 | tf_op jit(solution)/shard_map/all_to_all | solution.py:69
  28.6 16.4 %collective-permute-done.1.refs_2_ = bf16[256,768]{1,0:T(8,128)(2,1)S(1)} collective-permute-done((bf16[256,768]{1,0:T(8,128)(2,1)}, bf16[256,768]{1,0:T(8,128)(2,1)S(1)}, u32[]{:S(2)}, u32[]{:S(2)}) %collective-permute-start.1) | collective-permute-done | bytes 393248 | tf_op jit(solution)/shard_map/ppermute | solution.py:61
  65.8 9.6 %collective-permute-done.5 = bf16[128,768]{1,0:T(8,128)(2,1)S(1)} collective-permute-done((bf16[128,768]{1,0:T(8,128)(2,1)S(1)}, bf16[128,768]{1,0:T(8,128)(2,1)S(1)}, u32[]{:S(2)}, u32[]{:S(2)}) %collective-permute-start.5) | collective-permute-done | bytes 196640 | tf_op jit(solution)/shard_map/ppermute | solution.py:61
  79.9 7.4 %collective-permute-done.16 = bf16[192,768]{1,0:T(8,128)(2,1)S(1)} collective-permute-done((bf16[192,768]{1,0:T(8,128)(2,1)S(1)}, bf16[192,768]{1,0:T(8,128)(2,1)S(1)}, u32[]{:S(2)}, u32[]{:S(2)}) %collective-permute-start.16) | collective-permute-done | bytes 294944 | tf_op jit(solution)/shard_map/ppermute | solution.py:61
  87.3 14.3 %collective-permute-done.15 = bf16[192,768]{1,0:T(8,128)(2,1)S(1)} collective-permute-done((bf16[192,768]{1,0:T(8,128)(2,1)S(1)}, bf16[192,768]{1,0:T(8,128)(2,1)S(1)}, u32[]{:S(2)}, u32[]{:S(2)}) %collective-permute-start.15) | collective-permute-done | bytes 294944 | tf_op jit(solution)/shard_map/ppermute | solution.py:61
  107.6 29.0 %collective-permute-done.10.refs_4_.refs_12_ = bf16[3,128,768]{2,1,0:T(8,128)(2,1)S(1)} collective-permute-done((bf16[3,128,768]{2,1,0:T(8,128)(2,1)S(1)}, bf16[3,128,768]{2,1,0:T(8,128)(2,1)S(1)}, u32[]{:S(2)}, u32[]{:S(2)}) %collective-permute-start.10) | collective-permute-done | bytes 589856 | tf_op jit(solution)/shard_map/ppermute | solution.py:61
  149.6 7.2 %collective-permute-done.12.refs_6_.refs_14_ = bf16[3,128,768]{2,1,0:T(8,128)(2,1)} collective-permute-done((bf16[3,128,768]{2,1,0:T(8,128)(2,1)}, bf16[3,128,768]{2,1,0:T(8,128)(2,1)}, u32[]{:S(2)}, u32[]{:S(2)}) %collective-permute-start.12) | collective-permute-done | bytes 589856 | tf_op jit(solution)/shard_map/ppermute | solution.py:61
  156.8 5.8 %collective-permute-done.18.refs_2_ = bf16[3,192,768]{2,1,0:T(8,128)(2,1)} collective-permute-done((bf16[3,192,768]{2,1,0:T(8,128)(2,1)S(1)}, bf16[3,192,768]{2,1,0:T(8,128)(2,1)}, u32[]{:S(2)}, u32[]{:S(2)}) %collective-permute-start.18) | collective-permute-done | bytes 884768 | tf_op jit(solution)/shard_map/ppermute | solution.py:61
  162.6 17.5 %collective-permute-done.22.refs_6_ = bf16[3,192,768]{2,1,0:T(8,128)(2,1)} collective-permute-done((bf16[3,192,768]{2,1,0:T(8,128)(2,1)}, bf16[3,192,768]{2,1,0:T(8,128)(2,1)}, u32[]{:S(2)}, u32[]{:S(2)}) %collective-permute-start.22) | collective-permute-done | bytes 884768 | tf_op jit(solution)/shard_map/ppermute | solution.py:61
  185.7 11.1 %columns_forward.1 = (f32[256,768]{1,0:T(8,128)}, bf16[256,768]{1,0:T(8,128)(2,1)}, bf16[3,4,256,192]{3,2,1,0:T(8,128)(2,1)}, bf16[4,256,192]{2,1,0:T(8,128)(2,1)}, f32[256,768]{1,0:T(8,128)}) custom-call(s32[2]{0:T(128)} %pad_add_fusion.me_ref, bf16[256,768]{1,0:T(8,128)(2,1)} %bitcast.120, bf16[4,256,192]{2,1,0:T(8,128)(2,1)} %reshape.197.attended.refs_5_, ...), custom_call_target="tpu_custom_call" | custom-call | flops 1509949440 | bytes 20971520 | tf_op jit(solution)/shard_map/columns_forward/pallas_call | solution.py:80
  196.9 16.1 %feed_forward.1 = (bf16[256,768]{1,0:T(8,128)(2,1)}, f32[256,768]{1,0:T(8,128)}, f32[1,768]{1,0:T(1,128)}, bf16[4,4,96,768]{3,2,1,0:T(8,128)(2,1)}, bf16[4,4,96,...) custom-call(s32[2]{0:T(128)} %pad_add_fusion.me_ref, ...), custom_call_target="tpu_custom_call" | custom-call | flops 7247757312 | bytes 31457280 | tf_op jit(solution)/shard_map/feed_forward/pallas_call | solution.py:80
  213.9 20.0 %columns_backward.1 = (f32[256,768]{1,0:T(8,128)}, bf16[256,768]{1,0:T(8,128)(2,1)}, bf16[4,256,192]{2,1,0:T(8,128)(2,1)}, f32[1,768]{1,0:T(1,128)}, bf16[4,4,96...) custom-call(s32[2]{0:T(128)} %pad_add_fusion.me_ref, f32[256,768]{1,0:T(8,128)} %get-tuple-element.53.refs_0_, ...), custom_call_target="tpu_custom_call" | custom-call | flops 3019898880 | bytes 31457280 | tf_op jit(solution)/shard_map/columns_backward/pallas_call | solution.py:80
  250.0 8.0 %all-to-all-done.5.mixed_grad = bf16[16,32,512]{2,1,0:T(8,128)(2,1)S(1)} async-done(((bf16[16,32,512]{2,1,0:T(8,128)(2,1)}), bf16[16,32,512]{2,1,0:T(8,128)(2,1)S(1)}, u32[]{:S(2)}, u32[]{:S(2)}) %all-to-all-start.5) | async-done | bytes 524320 | tf_op jit(solution)/shard_map/all_to_all | solution.py:69
  258.8 7.5 %attend_back.1 = (bf16[8,64,512]{2,1,0:T(8,128)(2,1)}, f32[8,2,64,512]{3,2,1,0:T(8,128)}, bf16[8,2,64,512]{3,2,1,0:T(8,128)(2,1)}) custom-call(bf16[8,3,64,512]{3,2,1,0:T(8,128)(2,1)} %copy-done.16, bf16[8,3,64,512]{3,2,1,0:T(8,128)(2,1)} %collective-permute-done.3.other, f32[1,1024]{1,0:T(1,128)} %pad_maximum_fusion.6.key_ok, f32[512,1]{1,0:T(8,128)} %copy.34.weight, ...), custom_call_target="tpu_custom_call" | custom-call | flops 2684354560 | bytes 16777216 | tf_op jit(solution)/shard_map/attend_back/pallas_call | solution.py:80
  307.0 18.2 %collective-permute-done.28 = bf16[2,4,96,768]{3,2,1,0:T(8,128)(2,1)} collective-permute-done((bf16[2,4,96,768]{3,2,1,0:T(8,128)(2,1)}, bf16[2,4,96,768]{3,2,1,0:T(8,128)(2,1)}, u32[]{:S(2)}, u32[]{:S(2)}) %collective-permute-start.28) | collective-permute-done | bytes 1179680 | tf_op jit(solution)/shard_map/ppermute | solution.py:61
  329.9 24.9 %collective-permute-done.56 = bf16[1,4,96,768]{3,2,1,0:T(8,128)(2,1)S(1)} collective-permute-done((bf16[1,4,96,768]{3,2,1,0:T(8,128)(2,1)S(1)}, bf16[1,4,96,768]{3,2,1,0:T(8,128)(2,1)S(1)}, u32[]{:S(2)}, u32[]{:S(2)}) %collective-permute-start.56) | collective-permute-done | bytes 589856 | tf_op jit(solution)/shard_map/ppermute | solution.py:61
  372.2 19.5 %collective-permute-done.46 = f32[3,768]{1,0:T(4,128)S(1)} collective-permute-done((f32[3,768]{1,0:T(4,128)S(1)}, f32[3,768]{1,0:T(4,128)S(1)}, u32[]{:S(2)}, u32[]{:S(2)}) %collective-permute-start.46) | collective-permute-done | bytes 9248 | tf_op jit(solution)/shard_map/ppermute | solution.py:61
  410.7 7.0 %collective-permute-done.62 = bf16[96,768]{1,0:T(8,128)(2,1)S(1)} collective-permute-done((bf16[96,768]{1,0:T(8,128)(2,1)}, bf16[96,768]{1,0:T(8,128)(2,1)S(1)}, u32[]{:S(2)}, u32[]{:S(2)}) %collective-permute-start.62) | collective-permute-done | bytes 147488 | tf_op jit(solution)/shard_map/ppermute | solution.py:61
  419.6 13.6 %collective-permute-done.41.refs_12_ = bf16[3,80,768]{2,1,0:T(8,128)(2,1)S(1)} collective-permute-done((bf16[3,80,768]{2,1,0:T(8,128)(2,1)}, bf16[3,80,768]{2,1,0:T(8,128)(2,1)S(1)}, u32[]{:S(2)}, u32[]{:S(2)}) %collective-permute-start.41) | collective-permute-done | bytes 368672 | tf_op jit(solution)/shard_map/ppermute | solution.py:61
  445.9 6.2 %collective-permute-done.30.refs_1_ = bf16[576,256]{1,0:T(8,128)(2,1)S(1)} collective-permute-done((bf16[576,256]{1,0:T(8,128)(2,1)}, bf16[576,256]{1,0:T(8,128)(2,1)S(1)}, u32[]{:S(2)}, u32[]{:S(2)}) %collective-permute-start.30) | collective-permute-done | bytes 294944 | tf_op jit(solution)/shard_map/ppermute | solution.py:61
  454.4 10.9 %collective-permute-done.33.refs_2_ = bf16[576,256]{1,0:T(8,128)(2,1)S(1)} collective-permute-done((bf16[576,256]{1,0:T(8,128)(2,1)S(1)}, bf16[576,256]{1,0:T(8,128)(2,1)S(1)}, u32[]{:S(2)}, u32[]{:S(2)}) %collective-permute-start.33) | collective-permute-done | bytes 294944 | tf_op jit(solution)/shard_map/ppermute | solution.py:61
  465.3 9.1 %collective-permute-start.50 = (bf16[2,96,576]{2,1,0:T(8,128)(2,1)S(1)}, bf16[2,96,576]{2,1,0:T(8,128)(2,1)S(1)}, u32[]{:S(2)}, u32[]{:S(2)}) collective-permute-start(bf16[2,96,576]{2,1,0:T(8,128)(2,1)S(1)} %slice.161), channel_id=1, source_target_pairs={{0,16},{8,24},{16,0},{24,8},{1,17},{9,25},{17,1},{25,9},{2,18},{10... | collective-permute-start | bytes 663560 | tf_op jit(solution)/shard_map/ppermute | solution.py:61
  475.2 6.2 %finish.1 = bf16[256,768]{1,0:T(8,128)(2,1)} custom-call(s32[2]{0:T(128)} %pad_add_fusion.me_ref, bf16[576,256]{1,0:T(8,128)(2,1)} %get-tuple-element.71.refs_0_, bf16[576,256]{1,0:T(8,128)(2,1)} %copy-done.34, bf16[576,256]{1,0:T(8,128)(2,1)} %copy-done.35, bf16[576,256]{1,0:T(8,128)(2,1)} %copy-done.36, bf16[256,768]{1,0:T(8,128)(2,1)} %bitcast.118, ...), custom_call_target="tpu_custom_call" | custom-call | flops 905969664 | bytes 8388608 | tf_op jit(solution)/shard_map/finish/pallas_call | solution.py:80
  481.4 6.2 %collective-permute-done.54 = bf16[96,960]{1,0:T(8,128)(2,1)} collective-permute-done((bf16[96,960]{1,0:T(8,128)(2,1)S(1)}, bf16[96,960]{1,0:T(8,128)(2,1)}, u32[]{:S(2)}, u32[]{:S(2)}) %collective-permute-start.54) | collective-permute-done | bytes 184352 | tf_op jit(solution)/shard_map/ppermute | solution.py:61
  (306 shorter events, 195.4 us)
Async XLA Ops:
  9.9 35.1 %collective-permute-start.1 = (bf16[256,768]{1,0:T(8,128)(2,1)}, bf16[256,768]{1,0:T(8,128)(2,1)S(1)}, u32[]{:S(2)}, u32[]{:S(2)}) collective-permute-start(bf16[256,768]{1,0:T(8,128)(2,1)} %bitcast.115), channel_id=1, source_target_pairs={{0,2},{1,3},{2,0},{3,1},{4,6},{5,7},{6,4},{7,5},{8,10},{9,11},{10,... | collective-permute-start | bytes 1179656 | tf_op jit(solution)/shard_map/ppermute | solution.py:61
  79.9 60.3 %collective-permute-start.3 = (bf16[8,3,64,512]{3,2,1,0:T(8,128)(2,1)S(1)}, bf16[8,3,64,512]{3,2,1,0:T(8,128)(2,1)}, u32[]{:S(2)}, u32[]{:S(2)}) collective-permute-start(bf16[8,3,64,512]{3,2,1,0:T(8,128)(2,1)S(1)} %all-to-all-done.2.own), channel_id=1, source_target_pairs={{0,4},{4,0},{1,5},{5,1},{2,6},{6,2},{3,7},{7,3},{8,12},{12,8},{9,1... | collective-permute-start | bytes 4718600 | tf_op jit(solution)/shard_map/ppermute | solution.py:61
  103.6 33.9 %collective-permute-start.20 = (bf16[3,192,768]{2,1,0:T(8,128)(2,1)S(1)}, bf16[3,192,768]{2,1,0:T(8,128)(2,1)}, u32[]{:S(2)}, u32[]{:S(2)}) collective-permute-start(bf16[3,192,768]{2,1,0:T(8,128)(2,1)S(1)} %pad_maximum_fusion.2.refs_0_), channel_id=1, source_target_pairs={{0,16},{8,24},{16,0},{24,8},{1,17},{9,25},{17,1},{25,9},{2,18},{10... | collective-permute-start | bytes 2654216 | tf_op jit(solution)/shard_map/ppermute | solution.py:61
  137.5 42.6 %collective-permute-start.22 = (bf16[3,192,768]{2,1,0:T(8,128)(2,1)}, bf16[3,192,768]{2,1,0:T(8,128)(2,1)}, u32[]{:S(2)}, u32[]{:S(2)}) collective-permute-start(bf16[3,192,768]{2,1,0:T(8,128)(2,1)} %collective-permute-done.20.refs_4_), channel_id=1, source_target_pairs={{0,8},{8,0},{16,24},{24,16},{1,9},{9,1},{17,25},{25,17},{2,10},{10... | collective-permute-start | bytes 2654216 | tf_op jit(solution)/shard_map/ppermute | solution.py:61
  140.2 39.9 %collective-permute-start.9 = (bf16[3,128,768]{2,1,0:T(8,128)(2,1)}, bf16[3,128,768]{2,1,0:T(8,128)(2,1)}, u32[]{:S(2)}, u32[]{:S(2)}) collective-permute-start(bf16[3,128,768]{2,1,0:T(8,128)(2,1)} %collective-permute-done.8.refs_2_.refs_10_), channel_id=1, source_target_pairs={{0,4},{4,0},{1,5},{5,1},{2,6},{6,2},{3,7},{7,3},{8,12},{12,8},{9,1... | collective-permute-start | bytes 1769480 | tf_op jit(solution)/shard_map/ppermute | solution.py:61
  145.5 36.3 %all-to-all-start.3 = ((bf16[16,32,512]{2,1,0:T(8,128)(2,1)}), bf16[16,32,512]{2,1,0:T(8,128)(2,1)S(1)}, u32[]{:S(2)}, u32[]{:S(2)}) async-start(bf16[16,32,512]{2,1,0:T(8,128)(2,1)} %attend.1), calls=%async_computation.3 | async-start | bytes 1048576 | tf_op jit(solution)/shard_map/all_to_all | solution.py:69
  149.4 47.4 %collective-permute-start.17 = (bf16[3,192,768]{2,1,0:T(8,128)(2,1)S(1)}, bf16[3,192,768]{2,1,0:T(8,128)(2,1)}, u32[]{:S(2)}, u32[]{:S(2)}) collective-permute-start(bf16[3,192,768]{2,1,0:T(8,128)(2,1)S(1)} %pad_maximum_fusion.2.refs_0_), channel_id=1, source_target_pairs={{0,4},{4,0},{1,5},{5,1},{2,6},{6,2},{3,7},{7,3},{8,12},{12,8},{9,1... | collective-permute-start | bytes 2654216 | tf_op jit(solution)/shard_map/ppermute | solution.py:61
  156.8 40.0 %collective-permute-start.21 = (bf16[3,192,768]{2,1,0:T(8,128)(2,1)}, bf16[3,192,768]{2,1,0:T(8,128)(2,1)}, u32[]{:S(2)}, u32[]{:S(2)}) collective-permute-start(bf16[3,192,768]{2,1,0:T(8,128)(2,1)} %collective-permute-done.20.refs_4_), channel_id=1, source_target_pairs={{0,4},{4,0},{1,5},{5,1},{2,6},{6,2},{3,7},{7,3},{8,12},{12,8},{9,1... | collective-permute-start | bytes 2654216 | tf_op jit(solution)/shard_map/ppermute | solution.py:61
  162.6 34.3 %collective-permute-start.19 = (bf16[3,192,768]{2,1,0:T(8,128)(2,1)}, bf16[3,192,768]{2,1,0:T(8,128)(2,1)}, u32[]{:S(2)}, u32[]{:S(2)}) collective-permute-start(bf16[3,192,768]{2,1,0:T(8,128)(2,1)} %collective-permute-done.18.refs_2_), channel_id=1, source_target_pairs={{0,4},{4,0},{1,5},{5,1},{2,6},{6,2},{3,7},{7,3},{8,12},{12,8},{9,1... | collective-permute-start | bytes 2654216 | tf_op jit(solution)/shard_map/ppermute | solution.py:61
  213.0 34.5 %collective-permute-start.25 = (bf16[4,4,96,768]{3,2,1,0:T(8,128)(2,1)}, bf16[4,4,96,768]{3,2,1,0:T(8,128)(2,1)}, u32[]{:S(2)}, u32[]{:S(2)}) collective-permute-start(bf16[4,4,96,768]{3,2,1,0:T(8,128)(2,1)} %get-tuple-element.62), channel_id=1, source_target_pairs={{0,4},{4,0},{1,5},{5,1},{2,6},{6,2},{3,7},{7,3},{8,12},{12,8},{9,1... | collective-permute-start | bytes 7077896 | tf_op jit(solution)/shard_map/ppermute | solution.py:61
  242.7 58.1 %collective-permute-start.29 = (bf16[4,4,96,960]{3,2,1,0:T(8,128)(2,1)}, bf16[4,4,96,960]{3,2,1,0:T(8,128)(2,1)}, u32[]{:S(2)}, u32[]{:S(2)}) collective-permute-start(bf16[4,4,96,960]{3,2,1,0:T(8,128)(2,1)} %get-tuple-element.68), channel_id=1, source_target_pairs={{0,4},{4,0},{1,5},{5,1},{2,6},{6,2},{3,7},{7,3},{8,12},{12,8},{9,1... | collective-permute-start | bytes 8847368 | tf_op jit(solution)/shard_map/ppermute | solution.py:61
  288.2 103.5 %collective-permute-start.39 = (bf16[3,80,768]{2,1,0:T(8,128)(2,1)}, bf16[3,80,768]{2,1,0:T(8,128)(2,1)}, u32[]{:S(2)}, u32[]{:S(2)}) collective-permute-start(bf16[3,80,768]{2,1,0:T(8,128)(2,1)} %pad_maximum_fusion.4.refs_8_), channel_id=1, source_target_pairs={{0,8},{8,0},{16,24},{24,16},{1,9},{9,1},{17,25},{25,17},{2,10},{10... | collective-permute-start | bytes 1105928 | tf_op jit(solution)/shard_map/ppermute | solution.py:61
  289.9 35.3 %collective-permute-start.28 = (bf16[2,4,96,768]{3,2,1,0:T(8,128)(2,1)}, bf16[2,4,96,768]{3,2,1,0:T(8,128)(2,1)}, u32[]{:S(2)}, u32[]{:S(2)}) collective-permute-start(bf16[2,4,96,768]{3,2,1,0:T(8,128)(2,1)} %slice.156), channel_id=1, source_target_pairs={{0,8},{8,0},{16,24},{24,16},{1,9},{9,1},{17,25},{25,17},{2,10},{10... | collective-permute-start | bytes 3538952 | tf_op jit(solution)/shard_map/ppermute | solution.py:61
  293.7 64.6 %all-to-all-start.6 = ((bf16[8,3,64,512]{3,2,1,0:T(8,128)(2,1)}), bf16[8,3,64,512]{3,2,1,0:T(8,128)(2,1)}, u32[]{:S(2)}, u32[]{:S(2)}) async-start(bf16[8,3,64,512]{3,2,1,0:T(8,128)(2,1)} %pad_maximum_fusion.1), calls=%async_computation.6 | async-start | bytes 3145728 | tf_op jit(solution)/shard_map/all_to_all | solution.py:69
  298.7 56.0 %collective-permute-start.56 = (bf16[1,4,96,768]{3,2,1,0:T(8,128)(2,1)S(1)}, bf16[1,4,96,768]{3,2,1,0:T(8,128)(2,1)S(1)}, u32[]{:S(2)}, u32[]{:S(2)}) collective-permute-start(bf16[1,4,96,768]{3,2,1,0:T(8,128)(2,1)S(1)} %slice.176), channel_id=1, source_target_pairs={{0,8},{8,0},{16,24},{24,16},{1,9},{9,1},{17,25},{25,17},{2,10},{10... | collective-permute-start | bytes 1769480 | tf_op jit(solution)/shard_map/ppermute | solution.py:61
  305.5 90.6 %collective-permute-start.31 = (bf16[2,4,96,960]{3,2,1,0:T(8,128)(2,1)}, bf16[2,4,96,960]{3,2,1,0:T(8,128)(2,1)}, u32[]{:S(2)}, u32[]{:S(2)}) collective-permute-start(bf16[2,4,96,960]{3,2,1,0:T(8,128)(2,1)} %slice.158), channel_id=1, source_target_pairs={{0,8},{8,0},{16,24},{24,16},{1,9},{9,1},{17,25},{25,17},{2,10},{10... | collective-permute-start | bytes 4423688 | tf_op jit(solution)/shard_map/ppermute | solution.py:61
  328.7 38.3 %collective-permute-start.60 = (bf16[1,4,96,768]{3,2,1,0:T(8,128)(2,1)}, bf16[1,4,96,768]{3,2,1,0:T(8,128)(2,1)}, u32[]{:S(2)}, u32[]{:S(2)}) collective-permute-start(bf16[1,4,96,768]{3,2,1,0:T(8,128)(2,1)} %slice.182), channel_id=1, source_target_pairs={{0,16},{8,24},{16,0},{24,8},{1,17},{9,25},{17,1},{25,9},{2,18},{10... | collective-permute-start | bytes 1769480 | tf_op jit(solution)/shard_map/ppermute | solution.py:61
  356.5 36.7 %collective-permute-start.57 = (bf16[96,768]{1,0:T(8,128)(2,1)}, bf16[96,768]{1,0:T(8,128)(2,1)}, u32[]{:S(2)}, u32[]{:S(2)}) collective-permute-start(bf16[96,768]{1,0:T(8,128)(2,1)} %get-tuple-element.114), channel_id=1, source_target_pairs={{0,1},{1,0},{2,3},{3,2},{4,5},{5,4},{6,7},{7,6},{8,9},{9,8},{10,11... | collective-permute-start | bytes 442376 | tf_op jit(solution)/shard_map/ppermute | solution.py:61
  357.5 44.1 %collective-permute-start.59 = (bf16[96,768]{1,0:T(8,128)(2,1)}, bf16[96,768]{1,0:T(8,128)(2,1)}, u32[]{:S(2)}, u32[]{:S(2)}) collective-permute-start(bf16[96,768]{1,0:T(8,128)(2,1)} %get-tuple-element.115), channel_id=1, source_target_pairs={{0,3},{1,2},{2,1},{3,0},{4,7},{5,6},{6,5},{7,4},{8,11},{9,10},{10,... | collective-permute-start | bytes 442376 | tf_op jit(solution)/shard_map/ppermute | solution.py:61
  358.3 43.3 %all-to-all-start.4 = ((bf16[8,32,768]{2,1,0:T(8,128)(2,1)}), bf16[8,32,768]{2,1,0:T(8,128)(2,1)S(1)}, u32[]{:S(2)}, u32[]{:S(2)}) async-start(bf16[8,32,768]{2,1,0:T(8,128)(2,1)} %bitcast.131), calls=%async_computation.4 | async-start | bytes 786432 | tf_op jit(solution)/shard_map/all_to_all | solution.py:69
  400.6 38.5 %collective-permute-start.52 = (bf16[1,4,96,960]{3,2,1,0:T(8,128)(2,1)S(1)}, bf16[1,4,96,960]{3,2,1,0:T(8,128)(2,1)}, u32[]{:S(2)}, u32[]{:S(2)}) collective-permute-start(bf16[1,4,96,960]{3,2,1,0:T(8,128)(2,1)S(1)} %slice.165), channel_id=1, source_target_pairs={{0,16},{8,24},{16,0},{24,8},{1,17},{9,25},{17,1},{25,9},{2,18},{10... | collective-permute-start | bytes 2211848 | tf_op jit(solution)/shard_map/ppermute | solution.py:61
  401.7 72.7 %all-to-all-start.7 = ((bf16[8,32,768]{2,1,0:T(8,128)(2,1)}), bf16[8,32,768]{2,1,0:T(8,128)(2,1)S(1)}, u32[]{:S(2)}, u32[]{:S(2)}) async-start(bf16[8,32,768]{2,1,0:T(8,128)(2,1)} %bitcast.130), calls=%async_computation.7 | async-start | bytes 786432 | tf_op jit(solution)/shard_map/all_to_all | solution.py:69
  445.9 35.5 %collective-permute-start.53 = (bf16[96,960]{1,0:T(8,128)(2,1)}, bf16[96,960]{1,0:T(8,128)(2,1)}, u32[]{:S(2)}, u32[]{:S(2)}) collective-permute-start(bf16[96,960]{1,0:T(8,128)(2,1)} %get-tuple-element.108), channel_id=1, source_target_pairs={{0,1},{1,0},{2,3},{3,2},{4,5},{5,4},{6,7},{7,6},{8,9},{9,8},{10,11... | collective-permute-start | bytes 552968 | tf_op jit(solution)/shard_map/ppermute | solution.py:61
  454.2 33.5 %collective-permute-start.54 = (bf16[96,960]{1,0:T(8,128)(2,1)S(1)}, bf16[96,960]{1,0:T(8,128)(2,1)}, u32[]{:S(2)}, u32[]{:S(2)}) collective-permute-start(bf16[96,960]{1,0:T(8,128)(2,1)S(1)} %get-tuple-element.110), channel_id=1, source_target_pairs={{0,2},{1,3},{2,0},{3,1},{4,6},{5,7},{6,4},{7,5},{8,10},{9,11},{10,... | collective-permute-start | bytes 552968 | tf_op jit(solution)/shard_map/ppermute | solution.py:61
  (97 other events, 1744.6 us)
